TPU v7x, 32 devices: a whole 2x2x4 slice. The times are simulated.
32 devices in a mesh: seg: 8 (over z, y), sp: 4 (over x, core).
Axes of the slice: x: 2, y: 2, z: 4, core: 2. Of those that a mesh axis runs over, the one named last changes fastest.
Arguments:
- coeffs: float32 [8, 128, 680], P('sp', 'seg'), may hold values from -0.6 to 0.6
- points: float32 [3, 128, 768], P(None, 'seg'), may hold values from -1 to 1
- owner_leaf: int32 [128, 6], P('seg'), may hold values from 0 to 127, as said below
- reaction: float32 [8, 8], replicated, may hold values from -2 to 2
- fit_matrix: float32 [768, 680], replicated, may hold values from -0.21875 to 0.21875
- new_seg: int32 [128], replicated, may hold values from 0 to 7, as said below
- near_src: int32 [128, 16], replicated, may hold values from -1 to 127, as said below
- near_op: int32 [128, 16], replicated, may hold values from 0 to 1
- near_mat: bfloat16 [2, 680, 680], replicated, may hold values from -0.0546875 to 0.0546875
- up_mat: bfloat16 [680, 152], replicated, may hold values from -0.21875 to 0.21875
- far_src: int32 [128, 8], replicated, may hold values from -1 to 127, as said below
- trans_mat: bfloat16 [8, 152, 152], replicated, may hold values from -0.15625 to 0.15625
- down_mat: bfloat16 [152, 680], replicated, may hold values from -0.5 to 0.5
Outputs:
- updated: float32 [8, 192, 680], P('sp', 'seg')
Inputs may be any that keep to these rules, and one draw needn't show every extreme that they name: `owner_leaf`: of the 96 blocks of one segment's leaves, at most 24 have their owner among the 16 leaves of any one segment. `new_seg`: never falls along the leaves; leaf t goes to segment t // 16, or to the one before only if t % 16 < 4, or to the one after only if t % 16 >= 12. `near_src`: -1 marks an unused entry; any other entry differs from its row's leaf index by at most 4. `far_src`: -1 marks an absent interaction.
All inputs are finite; a program needn't handle non-finite values.
Results may differ from a plain program's by a relative error of at most 0.0035.
Values may be sent and summed in bfloat16 or wider, within the bound.
A program may use at most 64 MiB of HBM per device.

v0:
```python
import jax
import jax.numpy as jnp
import numpy as np
from jax import lax
from jax.sharding import PartitionSpec as P

ORDER = 14
NODES = 768
PB = 128
BLOCKS = 6
MOVE = 4
REACH = 4


precise = lax.Precision.HIGHEST


def extended(value, sides, width):
    for axis, dim in sides:
        size, length = (lax.axis_size(axis), value.shape[dim])
        up = [(i, (i + 1) % size) for i in range(size - 1)]
        down = [(j, i) for i, j in up]
        last = lax.slice_in_dim(value, length - width, length, axis=dim)
        first = lax.slice_in_dim(value, 0, width, axis=dim)
        before = lax.ppermute(last, axis, up)
        after = lax.ppermute(first, axis, down)
        value = jnp.concatenate([before, value, after], axis=dim)
    return value


def basis_tables(order):
    pair_list = [(deg_x, deg_y) for deg_x in range(order + 1) for deg_y in range(order + 1 - deg_x)]
    total_width = (order + 1) * (order + 2) * (order + 3) // 6
    lookup = np.full((len(pair_list), order + 1), total_width, np.int32)
    x_select = np.zeros((len(pair_list), order + 1), np.float32)
    y_select = np.zeros((len(pair_list), order + 1), np.float32)
    counter = 0
    for row_number, (deg_x, deg_y) in enumerate(pair_list):
        x_select[row_number, deg_x] = 1.0
        y_select[row_number, deg_y] = 1.0
        for deg_z in range(order + 1 - deg_x - deg_y):
            lookup[row_number, deg_z] = counter
            counter += 1
    return (lookup, x_select, y_select)


def chebyshev(position_values, order):
    polynomials = [jnp.ones_like(position_values), position_values]
    for degree in range(2, order + 1):
        polynomials.append(2.0 * position_values * polynomials[-1] - polynomials[-2])
    return jnp.stack(polynomials[: order + 1], axis=-2)


def evaluate(coefficient, coords):
    lookup, x_select, y_select = basis_tables(ORDER)
    padded = jnp.concatenate(
        [coefficient, jnp.zeros(coefficient.shape[:-1] + (1,), coefficient.dtype)], axis=-1
    )
    dense_coef = jnp.take(padded, jnp.asarray(lookup), axis=-1)
    along_x = chebyshev(coords[0], ORDER)
    along_y = chebyshev(coords[1], ORDER)
    along_z = chebyshev(coords[2], ORDER)
    inner_sum = jnp.einsum("sqk,kp->sqp", dense_coef, along_z, precision=precise)
    y_rows = jnp.einsum("qk,kp->qp", jnp.asarray(y_select), along_y, precision=precise)
    folded = jnp.einsum(
        "sqp,qk->skp", inner_sum * y_rows[None], jnp.asarray(x_select), precision=precise
    )
    return jnp.sum(folded * along_x[None], axis=1)


def evaluate_many(coef_rows, coords):
    return lax.map(
        lambda block_args: evaluate(block_args[0], block_args[1]),
        (coef_rows, coords),
        batch_size=16,
    )


def shards(
    coeffs,
    points,
    owner_leaf,
    reaction,
    fit_matrix,
    new_seg,
    near_src,
    near_op,
    near_mat,
    up_mat,
    far_src,
    trans_mat,
    down_mat,
):
    local_species, leaf_dev, coef_width = coeffs.shape
    segments = lax.axis_size("seg")
    segment = lax.axis_index("seg")
    block_count = leaf_dev * BLOCKS
    capacity = max(2, 2 * block_count // segments)
    coords = points.reshape(3, block_count, PB).transpose(1, 0, 2)
    flat_owner = owner_leaf.reshape(-1)
    target_dev = flat_owner // leaf_dev
    owned_leaf = flat_owner % leaf_dev
    onehot = (target_dev[:, None] == jnp.arange(segments, dtype=jnp.int32)[None, :]).astype(
        jnp.int32
    )
    earlier = jnp.sum((jnp.cumsum(onehot, axis=0) - onehot) * onehot, axis=1)
    position = target_dev * capacity + earlier
    by_leaf = jnp.transpose(coeffs, (1, 0, 2))
    slot_leaf = jnp.full((segments * capacity,), -1, jnp.int32).at[position].set(owned_leaf)
    received = lax.all_to_all(
        slot_leaf.reshape(segments, capacity), "seg", split_axis=0, concat_axis=0, tiled=True
    )
    sources, item_count = received.shape
    wanted = received.reshape(-1)
    picked = jnp.take(by_leaf, jnp.clip(wanted, 0, leaf_dev - 1), axis=0)
    picked = jnp.where((wanted >= 0)[:, None, None], picked, jnp.zeros_like(picked))
    fetched = lax.all_to_all(
        picked.reshape(sources, item_count, local_species, coef_width),
        "seg",
        split_axis=0,
        concat_axis=0,
        tiled=True,
    )
    values = evaluate_many(
        fetched.reshape(segments * capacity, local_species, coef_width)[position], coords
    )
    values = (
        values.reshape(leaf_dev, BLOCKS, local_species, PB)
        .transpose(2, 0, 1, 3)
        .reshape(local_species, leaf_dev, NODES)
    )
    gathered = lax.all_gather(values, "sp", axis=0, tiled=True)
    species_start = lax.axis_index("sp") * local_species
    my_rows = lax.dynamic_slice_in_dim(reaction, species_start, local_species, 0)
    mixing = jnp.einsum("sr,rln->sln", my_rows, gathered, precision=precise)
    reacted = values + jnp.tanh(mixing)
    refitted = jnp.einsum("sln,nc->slc", reacted, fit_matrix, precision=precise)
    ghosts = refitted.astype(jnp.bfloat16)
    equivalent = jnp.einsum(
        "slc,cq->slq", ghosts, up_mat, preferred_element_type=jnp.float32
    ).astype(jnp.bfloat16)
    margin = MOVE + REACH
    padded = extended(ghosts, (("seg", 1),), margin)
    slot_total = leaf_dev + 2 * MOVE
    leaf_total = new_seg.shape[0]
    target = segment * leaf_dev - MOVE + jnp.arange(slot_total, dtype=jnp.int32)
    inside = (target >= 0) & (target < leaf_total)
    clipped = jnp.clip(target, 0, leaf_total - 1)
    live_slot = inside & (new_seg[clipped] == segment)
    own_term = padded[:, margin - MOVE : margin - MOVE + slot_total].astype(jnp.float32)
    near_from = near_src[clipped]
    near_kind = near_op[clipped]
    near_ok = live_slot[:, None] & (near_from >= 0)
    near_count = near_from.shape[1]
    offset_rows = jnp.clip(near_from - (segment * leaf_dev - margin), 0, leaf_dev + 2 * margin - 1)
    picked = jnp.take(padded, offset_rows.reshape(-1), axis=1).reshape(
        local_species, slot_total, near_count, coef_width
    )
    operators = jnp.arange(near_mat.shape[0], dtype=jnp.int32)
    choose = ((near_kind[None, :, :] == operators[:, None, None]) & near_ok[None, :, :]).astype(
        jnp.bfloat16
    )
    grouped = jnp.einsum("ojq,sjqc->osjc", choose, picked, preferred_element_type=jnp.float32)
    near_term = jnp.einsum(
        "osjc,ocd->sjd", grouped, near_mat.astype(jnp.float32), precision=precise
    )
    far_from = far_src[clipped]
    far_ok = live_slot[:, None] & (far_from >= 0)
    empty_rows = jnp.zeros(
        (local_species, slot_total, far_from.shape[1], up_mat.shape[1]), jnp.bfloat16
    )
    block_piece = lax.all_gather(equivalent, "seg", axis=1, tiled=True)
    piece_rows = block_piece.shape[1]
    in_piece = far_ok & (far_from >= 0) & (far_from < piece_rows)
    taken_rows = jnp.take(block_piece, jnp.clip(far_from, 0, piece_rows - 1).reshape(-1), axis=1)
    taken_rows = taken_rows.reshape(empty_rows.shape)
    far_rows = empty_rows + jnp.where(
        in_piece[None, :, :, None], taken_rows, jnp.zeros_like(taken_rows)
    )
    local_expansion = jnp.einsum(
        "sjoq,oqr->sjr", far_rows, trans_mat, preferred_element_type=jnp.float32
    ).astype(jnp.bfloat16)
    far_term = jnp.einsum(
        "sjq,qc->sjc", local_expansion, down_mat, preferred_element_type=jnp.float32
    )
    total = own_term + near_term + far_term
    return jnp.where(live_slot[None, :, None], total, jnp.zeros_like(total))


def solution(mesh):
    placed = (
        P("sp", "seg", None),
        P(None, "seg", None),
        P("seg", None),
        P(),
        P(),
        P(),
        P(),
        P(),
        P(),
        P(),
        P(),
        P(),
        P(),
    )
    return jax.shard_map(
        shards, mesh=mesh, in_specs=placed, out_specs=P("sp", "seg", None), check_vma=False
    )
```

profile of v0, /device:TPU:0, one launch (start us, length us, event | category | flops | bytes accessed | tf_op | source)
XLA Modules:
  0.0 234.8 jit_solution(2222798164039807863)
XLA Ops:
  3.1 7.3 %all-to-all-start = ((s32[8,1,24]{2,1,0:T(1,128)}), s32[8,1,24]{2,1,0:T(1,128)S(1)}, u32[]{:S(2)}, u32[]{:S(2)}) async-start(s32[8,1,24]{2,1,0:T(1,128)} %all_to_all.9), calls=%async_computation | async-start | bytes 8192 | tf_op jit(solution)/shard_map/all_to_all | solution.py:110
  11.4 5.4 %all-to-all-done = s32[8,1,24]{2,1,0:T(1,128)S(1)} async-done(((s32[8,1,24]{2,1,0:T(1,128)}), s32[8,1,24]{2,1,0:T(1,128)S(1)}, u32[]{:S(2)}, u32[]{:S(2)}) %all-to-all-start) | async-done | bytes 800 | tf_op jit(solution)/shard_map/all_to_all | solution.py:110
  17.0 1.9 gather_fusion.2
  18.9 1.7 select_select_fusion
  20.6 3.7 %all-to-all-start.1 = ((f32[8,24,2,680]{3,2,1,0:T(2,128)}), f32[8,24,2,680]{3,2,1,0:T(2,128)S(1)}, u32[]{:S(2)}, u32[]{:S(2)}) async-start(f32[8,24,2,680]{3,2,1,0:T(2,128)} %select_select_fusion), calls=%async_computation.1 | async-start | bytes 2359296 | tf_op jit(solution)/shard_map/all_to_all | solution.py:117
  29.8 22.1 %all-to-all-done.1 = f32[8,24,2,680]{3,2,1,0:T(2,128)S(1)} async-done(((f32[8,24,2,680]{3,2,1,0:T(2,128)}), f32[8,24,2,680]{3,2,1,0:T(2,128)S(1)}, u32[]{:S(2)}, u32[]{:S(2)}) %all-to-all-start.1) | async-done | bytes 1044512 | tf_op jit(solution)/shard_map/all_to_all | solution.py:117
  51.9 2.1 gather_fusion.3
  54.0 123.5 %while.14 = (s32[]{:T(128)}, f32[6,16,2,128]{3,2,1,0:T(2,128)}, f32[6,16,2,680]{3,2,1,0:T(2,128)}, f32[6,16,3,128]{3,1,0,2:T(8,128)S(1)}, s32[]{:T(128)}, /*inde...) while((s32[]{:T(128)}, f32[6,16,2,128]{3,2,1,0:T(2,128)}, ...), condition=%wide.region_5.6_spmd.clone, body=%wide.region_3.5_spmd.sunk.clone.sunk | while | flops 222994432 | bytes 13164617 | solution.py:72
  57.4 6.5 %gather_fusion = f32[1800,16,2]{1,2,0:T(2,128)} fusion(f32[16,2,681]{0,1,2:T(2,128)S(1)} %concatenate.10, s32[2048]{0:T(1024)S(1)} %pad_clamp_fusion.7), kind=kCustom, calls=%fused_computation.clone.1 | custom fusion | bytes 468000 | tf_op jit(solution)/shard_map/while/body/eval_jaxpr/vmap(jit(_take))/gather | solution.py:59
  63.8 4.4 %copy.181 = f32[120,15,16,2]{1,0,3,2:T(8,128)} copy(f32[120,15,16,2]{2,3,1,0:T(2,128)} %bitcast.134) | data formatting | bytes 460800 | tf_op jit(solution)/shard_map/while/body/eval_jaxpr/vmap(jit(_take))/gather | solution.py:59
  68.2 3.4 %fusion.97 = f32[16,2,120,128]{3,2,1,0:T(8,128)S(1)} fusion(f32[120,15,16,2]{1,0,3,2:T(8,128)} %copy.181, f32[16,15,128,1]{2,0,1,3:T(8,128)S(1)} %bitcast.138), kind=kOutput, calls=%fused_computation.10.clone.1 | convolution fusion | flops 88473600 | bytes 2319360 | tf_op jit(solution)/shard_map/while/body/eval_jaxpr/vmap(sqk,kp->sqp)/dot_general | solution.py:63
  78.0 6.5 %gather_fusion = f32[1800,16,2]{1,2,0:T(2,128)} fusion(f32[16,2,681]{0,1,2:T(2,128)S(1)} %concatenate.10, s32[2048]{0:T(1024)S(1)} %pad_clamp_fusion.7), kind=kCustom, calls=%fused_computation.clone.1 | custom fusion | bytes 468000 | tf_op jit(solution)/shard_map/while/body/eval_jaxpr/vmap(jit(_take))/gather | solution.py:59
  84.4 4.4 %copy.181 = f32[120,15,16,2]{1,0,3,2:T(8,128)} copy(f32[120,15,16,2]{2,3,1,0:T(2,128)} %bitcast.134) | data formatting | bytes 460800 | tf_op jit(solution)/shard_map/while/body/eval_jaxpr/vmap(jit(_take))/gather | solution.py:59
  88.8 3.4 %fusion.97 = f32[16,2,120,128]{3,2,1,0:T(8,128)S(1)} fusion(f32[120,15,16,2]{1,0,3,2:T(8,128)} %copy.181, f32[16,15,128,1]{2,0,1,3:T(8,128)S(1)} %bitcast.138), kind=kOutput, calls=%fused_computation.10.clone.1 | convolution fusion | flops 88473600 | bytes 2319360 | tf_op jit(solution)/shard_map/while/body/eval_jaxpr/vmap(sqk,kp->sqp)/dot_general | solution.py:63
  98.5 6.5 %gather_fusion = f32[1800,16,2]{1,2,0:T(2,128)} fusion(f32[16,2,681]{0,1,2:T(2,128)S(1)} %concatenate.10, s32[2048]{0:T(1024)S(1)} %pad_clamp_fusion.7), kind=kCustom, calls=%fused_computation.clone.1 | custom fusion | bytes 468000 | tf_op jit(solution)/shard_map/while/body/eval_jaxpr/vmap(jit(_take))/gather | solution.py:59
  105.0 4.4 %copy.181 = f32[120,15,16,2]{1,0,3,2:T(8,128)} copy(f32[120,15,16,2]{2,3,1,0:T(2,128)} %bitcast.134) | data formatting | bytes 460800 | tf_op jit(solution)/shard_map/while/body/eval_jaxpr/vmap(jit(_take))/gather | solution.py:59
  109.4 3.4 %fusion.97 = f32[16,2,120,128]{3,2,1,0:T(8,128)S(1)} fusion(f32[120,15,16,2]{1,0,3,2:T(8,128)} %copy.181, f32[16,15,128,1]{2,0,1,3:T(8,128)S(1)} %bitcast.138), kind=kOutput, calls=%fused_computation.10.clone.1 | convolution fusion | flops 88473600 | bytes 2319360 | tf_op jit(solution)/shard_map/while/body/eval_jaxpr/vmap(sqk,kp->sqp)/dot_general | solution.py:63
  119.1 6.5 %gather_fusion = f32[1800,16,2]{1,2,0:T(2,128)} fusion(f32[16,2,681]{0,1,2:T(2,128)S(1)} %concatenate.10, s32[2048]{0:T(1024)S(1)} %pad_clamp_fusion.7), kind=kCustom, calls=%fused_computation.clone.1 | custom fusion | bytes 468000 | tf_op jit(solution)/shard_map/while/body/eval_jaxpr/vmap(jit(_take))/gather | solution.py:59
  125.6 4.4 %copy.181 = f32[120,15,16,2]{1,0,3,2:T(8,128)} copy(f32[120,15,16,2]{2,3,1,0:T(2,128)} %bitcast.134) | data formatting | bytes 460800 | tf_op jit(solution)/shard_map/while/body/eval_jaxpr/vmap(jit(_take))/gather | solution.py:59
  130.0 3.4 %fusion.97 = f32[16,2,120,128]{3,2,1,0:T(8,128)S(1)} fusion(f32[120,15,16,2]{1,0,3,2:T(8,128)} %copy.181, f32[16,15,128,1]{2,0,1,3:T(8,128)S(1)} %bitcast.138), kind=kOutput, calls=%fused_computation.10.clone.1 | convolution fusion | flops 88473600 | bytes 2319360 | tf_op jit(solution)/shard_map/while/body/eval_jaxpr/vmap(sqk,kp->sqp)/dot_general | solution.py:63
  139.7 6.5 %gather_fusion = f32[1800,16,2]{1,2,0:T(2,128)} fusion(f32[16,2,681]{0,1,2:T(2,128)S(1)} %concatenate.10, s32[2048]{0:T(1024)S(1)} %pad_clamp_fusion.7), kind=kCustom, calls=%fused_computation.clone.1 | custom fusion | bytes 468000 | tf_op jit(solution)/shard_map/while/body/eval_jaxpr/vmap(jit(_take))/gather | solution.py:59
  146.1 4.4 %copy.181 = f32[120,15,16,2]{1,0,3,2:T(8,128)} copy(f32[120,15,16,2]{2,3,1,0:T(2,128)} %bitcast.134) | data formatting | bytes 460800 | tf_op jit(solution)/shard_map/while/body/eval_jaxpr/vmap(jit(_take))/gather | solution.py:59
  150.5 3.4 %fusion.97 = f32[16,2,120,128]{3,2,1,0:T(8,128)S(1)} fusion(f32[120,15,16,2]{1,0,3,2:T(8,128)} %copy.181, f32[16,15,128,1]{2,0,1,3:T(8,128)S(1)} %bitcast.138), kind=kOutput, calls=%fused_computation.10.clone.1 | convolution fusion | flops 88473600 | bytes 2319360 | tf_op jit(solution)/shard_map/while/body/eval_jaxpr/vmap(sqk,kp->sqp)/dot_general | solution.py:63
  160.2 6.5 %gather_fusion = f32[1800,16,2]{1,2,0:T(2,128)} fusion(f32[16,2,681]{0,1,2:T(2,128)S(1)} %concatenate.10, s32[2048]{0:T(1024)S(1)} %pad_clamp_fusion.7), kind=kCustom, calls=%fused_computation.clone.1 | custom fusion | bytes 468000 | tf_op jit(solution)/shard_map/while/body/eval_jaxpr/vmap(jit(_take))/gather | solution.py:59
  166.7 4.4 %copy.181 = f32[120,15,16,2]{1,0,3,2:T(8,128)} copy(f32[120,15,16,2]{2,3,1,0:T(2,128)} %bitcast.134) | data formatting | bytes 460800 | tf_op jit(solution)/shard_map/while/body/eval_jaxpr/vmap(jit(_take))/gather | solution.py:59
  171.1 3.4 %fusion.97 = f32[16,2,120,128]{3,2,1,0:T(8,128)S(1)} fusion(f32[120,15,16,2]{1,0,3,2:T(8,128)} %copy.181, f32[16,15,128,1]{2,0,1,3:T(8,128)S(1)} %bitcast.138), kind=kOutput, calls=%fused_computation.10.clone.1 | convolution fusion | flops 88473600 | bytes 2319360 | tf_op jit(solution)/shard_map/while/body/eval_jaxpr/vmap(sqk,kp->sqp)/dot_general | solution.py:63
  178.4 6.8 %all_gather.6 = f32[8,16,768]{2,1,0:T(8,128)S(1)} all-gather(f32[2,16,768]{2,1,0:T(8,128)S(1)} %reshape.351), channel_id=1, replica_groups=mesh['seg'=8,'sp'=4] {'sp'}, dimensions={0}, use_global_device_ids=true | all-gather | bytes 491520 | tf_op jit(solution)/shard_map/all_gather | solution.py:132
  186.5 3.5 %fusion.26 = bf16[2,16,680]{2,1,0:T(8,128)(2,1)S(1)} fusion(f32[768,680]{0,1:T(8,128)} %param.22, f32[2,16,768]{2,1,0:T(8,128)S(1)} %reshape.351, f32[2,16,768]{2,0,1:T(2,128)S(1)} %fusion.34), kind=kOutput, calls=%fused_computation.116 | convolution fusion | flops 200586496 | bytes 2329088 | tf_op jit(solution)/shard_map/sln,nc->slc/dot_general | solution.py:137
  190.0 3.1 %collective-permute-start = (bf16[2,8,680]{2,1,0:T(8,128)(2,1)S(1)}, bf16[2,8,680]{2,1,0:T(8,128)(2,1)S(1)}, u32[]{:S(2)}, u32[]{:S(2)}) collective-permute-start(bf16[2,8,680]{2,1,0:T(8,128)(2,1)S(1)} %get-tuple-element.198), channel_id=1, source_target_pairs={{0,4},{4,8},{8,12},{12,16},{16,20},{20,24},{24,28},{1,5},{5,9},{9,... | collective-permute-start | bytes 65288 | tf_op jit(solution)/shard_map/ppermute | solution.py:25
  194.7 30.7 %all_gather.7 = bf16[2,128,152]{2,1,0:T(8,128)(2,1)S(1)} all-gather(bf16[2,16,152]{2,1,0:T(8,128)(2,1)S(1)} %convolution_convert_fusion), channel_id=1, replica_groups=mesh['seg'=8,'sp'=4] {'seg'}, dimensions={1}, use_global_device_ids=true | all-gather | bytes 87552 | tf_op jit(solution)/shard_map/all_gather | solution.py:172
  225.5 1.8 gather_fusion.8
  227.4 4.5 %gather_fusion.5 = bf16[384,2,680]{2,1,0:T(2,128)(2,1)S(1)} fusion(bf16[2,32,680]{2,0,1:T(2,128)(2,1)S(1)} %copy.122, s32[1024]{0:T(1024)S(1)} %pad_clamp_fusion.2), kind=kCustom, calls=%fused_computation.5 | custom fusion | bytes 2090496 | tf_op jit(solution)/shard_map/jit(_take)/gather | solution.py:156
  (395 shorter events, 52.7 us)
Async XLA Ops:
  0.0 232.3 %copy-start = (bf16[2,680,680]{2,1,0:T(8,128)(2,1)S(1)}, bf16[2,680,680]{2,1,0:T(8,128)(2,1)}, u32[]{:S(2)}) copy-start(bf16[2,680,680]{2,1,0:T(8,128)(2,1)} %param.26) | copy-start | bytes 5548804
  3.1 13.7 %all-to-all-start = ((s32[8,1,24]{2,1,0:T(1,128)}), s32[8,1,24]{2,1,0:T(1,128)S(1)}, u32[]{:S(2)}, u32[]{:S(2)}) async-start(s32[8,1,24]{2,1,0:T(1,128)} %all_to_all.9), calls=%async_computation | async-start | bytes 8192 | tf_op jit(solution)/shard_map/all_to_all | solution.py:110
  20.6 4.7 %copy-start.15 = (s32[128,16]{0,1:T(8,128)S(1)}, s32[128,16]{0,1:T(8,128)}, u32[]{:S(2)}) copy-start(s32[128,16]{0,1:T(8,128)} %param.24) | copy-start | bytes 24580
  20.6 4.8 %copy-start.1 = (s32[128]{0:T(128)S(1)}, s32[128]{0:T(128)}, u32[]{:S(2)}) copy-start(s32[128]{0:T(128)} %param.23) | copy-start | bytes 1540
  20.6 6.9 %copy-start.16 = (s32[128,16]{0,1:T(8,128)S(1)}, s32[128,16]{0,1:T(8,128)}, u32[]{:S(2)}) copy-start(s32[128,16]{0,1:T(8,128)} %param.25) | copy-start | bytes 24580
  20.6 7.6 %copy-start.17 = (s32[128,8]{0,1:T(8,128)S(1)}, s32[128,8]{0,1:T(8,128)}, u32[]{:S(2)}) copy-start(s32[128,8]{0,1:T(8,128)} %param.28) | copy-start | bytes 12292
  20.6 31.2 %all-to-all-start.1 = ((f32[8,24,2,680]{3,2,1,0:T(2,128)}), f32[8,24,2,680]{3,2,1,0:T(2,128)S(1)}, u32[]{:S(2)}, u32[]{:S(2)}) async-start(f32[8,24,2,680]{3,2,1,0:T(2,128)} %select_select_fusion), calls=%async_computation.1 | async-start | bytes 2359296 | tf_op jit(solution)/shard_map/all_to_all | solution.py:117
  24.4 29.6 %copy-start.11 = (f32[120,15,1,1]{0,1,3,2:T(8,128)S(1)}, f32[120,15,1,1]{0,1,3,2:T(8,128)}, u32[]{:S(2)}) copy-start(f32[120,15,1,1]{0,1,3,2:T(8,128)} %constant.603) | copy-start | bytes 21604
  24.4 29.6 %copy-start.12 = (f32[120,15,1]{0,1,2:T(8,128)S(1)}, f32[120,15,1]{0,1,2:T(8,128)}, u32[]{:S(2)}) copy-start(f32[120,15,1]{0,1,2:T(8,128)} %constant.605) | copy-start | bytes 21604
  24.4 29.6 %copy-start.13 = (s32[1800]{0:T(1024)S(1)}, s32[1800]{0:T(1024)}, u32[]{:S(2)}) copy-start(s32[1800]{0:T(1024)} %constant.604) | copy-start | bytes 21604
  63.8 4.4 %copy-start.3 = (f32[16,15,128]{2,0,1:T(8,128)S(1)}, f32[16,15,128]{2,0,1:T(8,128)}, u32[]{:S(2)}) copy-start(f32[16,15,128]{2,0,1:T(8,128)} %copy-done.2) | copy-start | bytes 368644 | tf_op jit(solution)/shard_map/while
  68.2 3.4 %copy-start.5 = (f32[16,15,128]{2,0,1:T(8,128)S(1)}, f32[16,15,128]{2,0,1:T(8,128)}, u32[]{:S(2)}) copy-start(f32[16,15,128]{2,0,1:T(8,128)} %copy-done.4) | copy-start | bytes 368644 | tf_op jit(solution)/shard_map/while
  68.2 4.4 %copy-start.7 = (f32[16,15,128]{2,0,1:T(8,128)S(1)}, f32[16,15,128]{2,0,1:T(8,128)}, u32[]{:S(2)}) copy-start(f32[16,15,128]{2,0,1:T(8,128)} %copy-done.6) | copy-start | bytes 368644 | tf_op jit(solution)/shard_map/while
  84.4 4.4 %copy-start.3 = (f32[16,15,128]{2,0,1:T(8,128)S(1)}, f32[16,15,128]{2,0,1:T(8,128)}, u32[]{:S(2)}) copy-start(f32[16,15,128]{2,0,1:T(8,128)} %copy-done.2) | copy-start | bytes 368644 | tf_op jit(solution)/shard_map/while
  88.8 3.4 %copy-start.5 = (f32[16,15,128]{2,0,1:T(8,128)S(1)}, f32[16,15,128]{2,0,1:T(8,128)}, u32[]{:S(2)}) copy-start(f32[16,15,128]{2,0,1:T(8,128)} %copy-done.4) | copy-start | bytes 368644 | tf_op jit(solution)/shard_map/while
  88.8 4.4 %copy-start.7 = (f32[16,15,128]{2,0,1:T(8,128)S(1)}, f32[16,15,128]{2,0,1:T(8,128)}, u32[]{:S(2)}) copy-start(f32[16,15,128]{2,0,1:T(8,128)} %copy-done.6) | copy-start | bytes 368644 | tf_op jit(solution)/shard_map/while
  105.0 4.4 %copy-start.3 = (f32[16,15,128]{2,0,1:T(8,128)S(1)}, f32[16,15,128]{2,0,1:T(8,128)}, u32[]{:S(2)}) copy-start(f32[16,15,128]{2,0,1:T(8,128)} %copy-done.2) | copy-start | bytes 368644 | tf_op jit(solution)/shard_map/while
  109.4 3.4 %copy-start.5 = (f32[16,15,128]{2,0,1:T(8,128)S(1)}, f32[16,15,128]{2,0,1:T(8,128)}, u32[]{:S(2)}) copy-start(f32[16,15,128]{2,0,1:T(8,128)} %copy-done.4) | copy-start | bytes 368644 | tf_op jit(solution)/shard_map/while
  109.4 4.4 %copy-start.7 = (f32[16,15,128]{2,0,1:T(8,128)S(1)}, f32[16,15,128]{2,0,1:T(8,128)}, u32[]{:S(2)}) copy-start(f32[16,15,128]{2,0,1:T(8,128)} %copy-done.6) | copy-start | bytes 368644 | tf_op jit(solution)/shard_map/while
  125.5 4.4 %copy-start.3 = (f32[16,15,128]{2,0,1:T(8,128)S(1)}, f32[16,15,128]{2,0,1:T(8,128)}, u32[]{:S(2)}) copy-start(f32[16,15,128]{2,0,1:T(8,128)} %copy-done.2) | copy-start | bytes 368644 | tf_op jit(solution)/shard_map/while
  129.9 3.4 %copy-start.5 = (f32[16,15,128]{2,0,1:T(8,128)S(1)}, f32[16,15,128]{2,0,1:T(8,128)}, u32[]{:S(2)}) copy-start(f32[16,15,128]{2,0,1:T(8,128)} %copy-done.4) | copy-start | bytes 368644 | tf_op jit(solution)/shard_map/while
  129.9 4.4 %copy-start.7 = (f32[16,15,128]{2,0,1:T(8,128)S(1)}, f32[16,15,128]{2,0,1:T(8,128)}, u32[]{:S(2)}) copy-start(f32[16,15,128]{2,0,1:T(8,128)} %copy-done.6) | copy-start | bytes 368644 | tf_op jit(solution)/shard_map/while
  146.1 4.4 %copy-start.3 = (f32[16,15,128]{2,0,1:T(8,128)S(1)}, f32[16,15,128]{2,0,1:T(8,128)}, u32[]{:S(2)}) copy-start(f32[16,15,128]{2,0,1:T(8,128)} %copy-done.2) | copy-start | bytes 368644 | tf_op jit(solution)/shard_map/while
  150.5 3.4 %copy-start.5 = (f32[16,15,128]{2,0,1:T(8,128)S(1)}, f32[16,15,128]{2,0,1:T(8,128)}, u32[]{:S(2)}) copy-start(f32[16,15,128]{2,0,1:T(8,128)} %copy-done.4) | copy-start | bytes 368644 | tf_op jit(solution)/shard_map/while
  150.5 4.4 %copy-start.7 = (f32[16,15,128]{2,0,1:T(8,128)S(1)}, f32[16,15,128]{2,0,1:T(8,128)}, u32[]{:S(2)}) copy-start(f32[16,15,128]{2,0,1:T(8,128)} %copy-done.6) | copy-start | bytes 368644 | tf_op jit(solution)/shard_map/while
  166.7 4.4 %copy-start.3 = (f32[16,15,128]{2,0,1:T(8,128)S(1)}, f32[16,15,128]{2,0,1:T(8,128)}, u32[]{:S(2)}) copy-start(f32[16,15,128]{2,0,1:T(8,128)} %copy-done.2) | copy-start | bytes 368644 | tf_op jit(solution)/shard_map/while
  171.1 3.4 %copy-start.5 = (f32[16,15,128]{2,0,1:T(8,128)S(1)}, f32[16,15,128]{2,0,1:T(8,128)}, u32[]{:S(2)}) copy-start(f32[16,15,128]{2,0,1:T(8,128)} %copy-done.4) | copy-start | bytes 368644 | tf_op jit(solution)/shard_map/while
  171.1 4.4 %copy-start.7 = (f32[16,15,128]{2,0,1:T(8,128)S(1)}, f32[16,15,128]{2,0,1:T(8,128)}, u32[]{:S(2)}) copy-start(f32[16,15,128]{2,0,1:T(8,128)} %copy-done.6) | copy-start | bytes 368644 | tf_op jit(solution)/shard_map/while
  178.3 16.1 %copy-start.10 = (bf16[680,152]{0,1:T(8,128)(2,1)S(1)}, bf16[680,152]{0,1:T(8,128)(2,1)}, u32[]{:S(2)}) copy-start(bf16[680,152]{0,1:T(8,128)(2,1)} %param.27) | copy-start | bytes 620164
  190.0 37.2 %collective-permute-start = (bf16[2,8,680]{2,1,0:T(8,128)(2,1)S(1)}, bf16[2,8,680]{2,1,0:T(8,128)(2,1)S(1)}, u32[]{:S(2)}, u32[]{:S(2)}) collective-permute-start(bf16[2,8,680]{2,1,0:T(8,128)(2,1)S(1)} %get-tuple-element.198), channel_id=1, source_target_pairs={{0,4},{4,8},{8,12},{12,16},{16,20},{20,24},{24,28},{1,5},{5,9},{9,... | collective-permute-start | bytes 65288 | tf_op jit(solution)/shard_map/ppermute | solution.py:25
  193.2 34.1 %collective-permute-start.1 = (bf16[2,8,680]{2,1,0:T(8,128)(2,1)S(1)}, bf16[2,8,680]{2,1,0:T(8,128)(2,1)S(1)}, u32[]{:S(2)}, u32[]{:S(2)}) collective-permute-start(bf16[2,8,680]{2,1,0:T(8,128)(2,1)S(1)} %get-tuple-element.199), channel_id=1, source_target_pairs={{4,0},{8,4},{12,8},{16,12},{20,16},{24,20},{28,24},{5,1},{9,5},{13... | collective-permute-start | bytes 65288 | tf_op jit(solution)/shard_map/ppermute | solution.py:26
  194.7 37.2 %copy-start.18 = (pred[24,16]{1,0:T(8,128)(4,1)S(1)}, pred[24,16]{1,0:T(8,128)(4,1)}, u32[]{:S(2)}) copy-start(pred[24,16]{1,0:T(8,128)(4,1)} %get-tuple-element.200) | copy-start | bytes 1156
  (34 other events, 32.3 us)
where the time goes:
time: 236 us; the launch traced here: 235 us
  local copies, waits for them, and re-layouts  105 us (44%)
  matrix products  41.4 us (18%)
  blocking collectives  37.5 us (16%)
  waiting for transfers between devices  27.6 us (12%)
  starting transfers between devices  15.5 us (7%)
  other arithmetic  6.43 us (3%)
    gather x12, local copies, waits for them, and re-layouts, evaluate(): dense_coef = jnp.take(padded, jnp.asarray(lookup), axis=-1)  65.1 us
    all_gather x1, blocking collectives, shards(): block_piece = lax.all_gather(equivalent, 'seg', axis=1, tiled=True)  30.7 us
    all_to_all x1, waiting for transfers between devices, shards(): lax.all_to_all(picked.reshape(sources, item_count, local_species, coef_wi...  22.1 us
    dot_general x6, matrix products, evaluate(): jnp.einsum('sqk,kp->sqp', dense_coef, along_z, precision=precise)  20.5 us
    dynamic_slice x12, local copies, waits for them, and re-layouts, evaluate_many(): lax.map(lambda block_args: evaluate(block_args[0], block_args[1]), (coef_...  10.8 us
    dot_general x6, matrix products, evaluate(): jnp.einsum('sqp,qk->skp', inner_sum * y_rows[None], jnp.asarray(x_select)...  7.35 us
    all_to_all x1, starting transfers between devices, shards(): lax.all_to_all(slot_leaf.reshape(segments, capacity), 'seg', split_axis=0...  7.31 us
    all_gather x1, blocking collectives, shards(): gathered = lax.all_gather(values, 'sp', axis=0, tiled=True)  6.79 us
  transfers between devices with their start and end apart: 4, of which 2 were waited for; matrix products, arithmetic and copies ran while one was open for 4% of the time, Pallas kernels for 0%

commit v1 on v0

v1 whole, which is shorter than its diff:
```python
import functools

import jax
import jax.numpy as jnp
import numpy as np
from jax import lax
from jax.experimental import pallas as pl
from jax.experimental.pallas import tpu as pltpu
from jax.sharding import PartitionSpec as P

ORDER = 14
PB = 128
MOVE = 4
REACH = 4
MESH = pl.DeviceIdType.MESH
VMEM = pl.BlockSpec(memory_space=pltpu.VMEM)
SMEM = pl.BlockSpec(memory_space=pltpu.SMEM)
ANY = pl.BlockSpec(memory_space=pl.ANY)
LIMIT = 60 * 1024 * 1024


def run_starts():
    starts, counter = {}, 0
    for i in range(ORDER + 1):
        for j in range(ORDER + 1 - i):
            starts[i, j] = counter
            counter += ORDER + 1 - i - j
    return starts, counter


GROUPS = [(i, 0) for i in range(ORDER + 1)] + [(i, 1) for i in range(ORDER + 1 - 8)]
ROWS = 8 * len(GROUPS)


def remote(src, dst, send, recv, axis, to):
    return pltpu.make_async_remote_copy(
        src_ref=src, dst_ref=dst, send_sem=send, recv_sem=recv,
        device_id={axis: to}, device_id_type=MESH,
    )


def greet(axis, others):
    barrier = pltpu.get_barrier_semaphore()
    for to in others:
        pl.semaphore_signal(barrier, inc=1, device_id={axis: to}, device_id_type=MESH)
    pl.semaphore_wait(barrier, len(others))


def pair_gather_kernel(axis, n, src, out, send, recv, local):
    me = lax.axis_index(axis)
    half = n // 2
    partner = me + 1 - 2 * lax.rem(me, 2)
    ahead = [lax.rem(me + 2 * p, n) for p in range(half)]
    behind = [lax.rem(me + n - 2 * p, n) for p in range(half)]
    partner_behind = [lax.rem(partner + n - 2 * p, n) for p in range(half)]
    greet(axis, ahead[1:] + [partner])
    own = pltpu.make_async_copy(src, out.at[me], local)
    own.start()
    copies = []
    for p in range(1, half):
        copies.append(remote(src, out.at[me], send.at[p], recv.at[p], axis, ahead[p]))
        copies[-1].start()
    copies.append(remote(src, out.at[me], send.at[half], recv.at[half], axis, partner))
    copies[-1].start()
    for p in range(1, half):
        slot = out.at[behind[p]]
        remote(slot, slot, send.at[p], recv.at[p], axis, partner).wait_recv()
        copies.append(remote(slot, slot, send.at[half + p], recv.at[half + p], axis, partner))
        copies[-1].start()
    for p in range(half):
        slot = out.at[partner_behind[p]]
        remote(slot, slot, send.at[half + p], recv.at[half + p], axis, partner).wait_recv()
    for copy in copies:
        copy.wait_send()
    own.wait()


def pair_gather(value, axis, collective_id):
    n = lax.axis_size(axis)
    return pl.pallas_call(
        functools.partial(pair_gather_kernel, axis, n),
        out_shape=jax.ShapeDtypeStruct((n,) + value.shape, value.dtype),
        in_specs=[ANY],
        out_specs=ANY,
        scratch_shapes=[
            pltpu.SemaphoreType.DMA((n,)),
            pltpu.SemaphoreType.DMA((n,)),
            pltpu.SemaphoreType.DMA,
        ],
        compiler_params=pltpu.CompilerParams(
            collective_id=collective_id, has_side_effects=True
        ),
        name="gather_" + axis,
    )(value)


def evaluate_kernel(owner, coef, points, values, rows, dense, cheb):
    leaf_dev, blocks = owner.shape
    species = values.shape[0]
    width = coef.shape[2]
    starts, _ = run_starts()
    chunk = 8 // species
    for axis in range(3):
        for m in range(blocks):
            for h in range(leaf_dev // 8):
                x = points[axis, 8 * h : 8 * h + 8, PB * m : PB * m + PB]
                first = 16 * (m * leaf_dev + 8 * h)
                below, here = jnp.ones_like(x), x
                cheb[axis, pl.ds(first, 8, stride=16), :] = below
                for d in range(1, ORDER + 1):
                    cheb[axis, pl.ds(first + d, 8, stride=16), :] = here
                    below, here = here, 2.0 * x * here - below
                cheb[axis, pl.ds(first + ORDER + 1, 8, stride=16), :] = jnp.zeros_like(x)
    lane = lax.broadcasted_iota(jnp.int32, (8, 128), 1)

    def expand(c, carry):
        for k in range(chunk):
            b = c * chunk + k
            leaf = owner[lax.rem(b, leaf_dev), lax.div(b, leaf_dev)]
            rows[species * k : species * (k + 1), :width] = coef[leaf]
        tiles = []
        for t in range(rows.shape[1] // 128):
            x = rows[:, 128 * t : 128 * t + 128]
            x_high = x.astype(jnp.bfloat16).astype(jnp.float32)
            tiles.append((x_high, x - x_high))
        zero = jnp.zeros((8, 128), jnp.float32)
        for g, (i, upper) in enumerate(GROUPS):
            for k in range(8):
                j = 8 * upper + k
                if i + j > ORDER:
                    piece = zero
                else:
                    length = ORDER + 1 - i - j
                    t, shift = divmod(starts[i, j], 128)
                    parts = []
                    for kind in range(2):
                        turn = (128 - shift + 16 * kind) % 128
                        part = tiles[t][kind]
                        if turn:
                            part = pltpu.roll(part, turn, 1)
                        if shift + length > 128:
                            rest = pltpu.roll(tiles[t + 1][kind], turn, 1)
                            part = jnp.where(lane < 128 - shift + 16 * kind, part, rest)
                        parts.append(part)
                    second = jnp.where((lane >= 16) & (lane < 16 + length), parts[1], zero)
                    piece = jnp.where(lane < length, parts[0], second)
                dense[pl.ds(c * (8 * ROWS) + 8 * g + k, 8, stride=ROWS), :] = piece
        return carry

    lax.fori_loop(0, leaf_dev * blocks // chunk, expand, 0)

    def block(b):
        lhs = dense[pl.ds(b * (species * ROWS), species * ROWS), 0:32].astype(jnp.bfloat16)
        tx = cheb[0, pl.ds(b * 16, 16), :]
        ty = cheb[1, pl.ds(b * 16, 16), :]
        tz = cheb[2, pl.ds(b * 16, 16), :]
        high = tz.astype(jnp.bfloat16)
        tz_high = high.astype(jnp.float32)
        rhs = jnp.concatenate(
            [
                jnp.concatenate([tz_high, tz - tz_high], axis=1),
                jnp.concatenate([tz_high, jnp.zeros_like(tz)], axis=1),
            ],
            axis=0,
        ).astype(jnp.bfloat16)
        both = jnp.dot(lhs, rhs, preferred_element_type=jnp.float32)
        inner = both[:, :PB] + both[:, PB:]
        for s in range(species):
            total = [None, None]
            for g, (i, upper) in enumerate(GROUPS):
                r = s * ROWS + 8 * g
                term = inner[r : r + 8] * tx[i : i + 1]
                total[upper] = term if total[upper] is None else total[upper] + term
            summed = total[0] * ty[0:8] + total[1] * ty[8:16]
            values[s, pl.ds(b, 1), :] = jnp.sum(summed, axis=0, keepdims=True)

    def pair(c, carry):
        for k in range(4):
            block(4 * c + k)
        return carry

    lax.fori_loop(0, leaf_dev * blocks // 4, pair, 0)


def split(x):
    high = x.astype(jnp.bfloat16)
    return high, (x - high.astype(jnp.float32)).astype(jnp.bfloat16)


def refit_kernel(reaction, own, gathered, fit, up, ghosts, equivalent, reacted):
    species, block_count, _ = own.shape
    leaf_dev = equivalent.shape[0] // species
    blocks = block_count // leaf_dev
    total_species = reaction.shape[1]
    start = lax.axis_index("sp") * species
    for s in range(species):
        mixing = jnp.zeros((block_count, PB), jnp.float32)
        for r in range(total_species):
            other = gathered[r // species, r % species].astype(jnp.float32)
            mixing = mixing + reaction[start + s, r] * other
        result = own[s] + jnp.tanh(mixing)
        for m in range(blocks):
            reacted[s * leaf_dev : (s + 1) * leaf_dev, m * PB : (m + 1) * PB] = result[
                m * leaf_dev : (m + 1) * leaf_dev
            ]
    high, low = split(reacted[...])
    fit_high, fit_low = split(fit[...])
    main = jnp.dot(
        jnp.concatenate([high, low], axis=0), fit_high, preferred_element_type=jnp.float32
    )
    rest = jnp.dot(high, fit_low, preferred_element_type=jnp.float32)
    count = species * leaf_dev
    refitted = main[:count] + (main[count:] + rest)
    rounded = refitted.astype(jnp.bfloat16)
    half = leaf_dev // 2
    for s in range(species):
        for h in range(2):
            first = s * leaf_dev + h * half
            ghosts[h, s] = refitted[first : first + half].astype(jnp.bfloat16)
    equivalent[...] = jnp.dot(
        rounded, up[...], preferred_element_type=jnp.float32
    ).astype(jnp.bfloat16)


def exchange_kernel(n, ghosts, equivalent, before, after, everyone, send, recv, local):
    me = lax.axis_index("seg")
    ahead = [lax.rem(me + p, n) for p in range(n)]
    behind = [lax.rem(me + n - p, n) for p in range(n)]
    greet("seg", ahead[1:])
    own = pltpu.make_async_copy(equivalent, everyone.at[me], local)
    own.start()
    up = remote(ghosts.at[1], before, send.at[0], recv.at[0], "seg", ahead[1])
    down = remote(ghosts.at[0], after, send.at[n], recv.at[n], "seg", behind[1])
    up.start()
    down.start()
    copies = []
    for p in range(1, n):
        copies.append(
            remote(equivalent, everyone.at[me], send.at[p], recv.at[p], "seg", ahead[p])
        )
        copies[-1].start()
    for p in range(1, n):
        slot = everyone.at[behind[p]]
        remote(slot, slot, send.at[p], recv.at[p], "seg", ahead[p]).wait_recv()
    for copy in copies:
        copy.wait_send()
    up.wait()
    down.wait()
    own.wait()


def finish_kernel(
    table, ghosts, before, after, everyone, near_mat, trans, down, out, near_count, far_count
):
    species, slots, width = out.shape
    half = ghosts.shape[2]
    leaf_dev = 2 * half
    me = lax.axis_index("seg")
    n = everyone.shape[0]
    margin = MOVE + REACH
    near_ops = near_mat.shape[0]
    far_ops = trans.shape[0]
    rows = table[pl.ds(pl.multiple_of(me * leaf_dev, 8), slots), :]
    live = rows[:, 0:1] == me
    base = me * leaf_dev - margin
    seen = leaf_dev + 2 * margin
    near_lane = lax.broadcasted_iota(jnp.int32, (slots, seen), 1)
    slot_row = lax.broadcasted_iota(jnp.int32, (slots, seen), 0)
    near_from = rows[:, 1 : 1 + near_count]
    near_kind = rows[:, 1 + near_count : 1 + 2 * near_count]
    far_from = rows[:, 1 + 2 * near_count : 1 + 2 * near_count + far_count]
    near_from = jnp.where(live & (near_from >= 0), near_from - base, -1)
    far_from = jnp.where(live & (far_from >= 0), far_from, -1)
    weights = [((near_lane == slot_row + REACH) & live).astype(jnp.float32)]
    weights += [jnp.zeros((slots, seen), jnp.float32) for _ in range(near_ops)]
    for q in range(near_count):
        hit = near_lane == near_from[:, q : q + 1]
        for o in range(near_ops):
            chosen = hit & (near_kind[:, q : q + 1] == o)
            weights[1 + o] = weights[1 + o] + chosen.astype(jnp.float32)
    weights = jnp.concatenate(weights, axis=0).astype(jnp.bfloat16)
    leaf_total = n * leaf_dev
    far_lane = lax.broadcasted_iota(jnp.int32, (slots, leaf_total), 1)
    picks = jnp.concatenate(
        [(far_lane == far_from[:, o : o + 1]).astype(jnp.float32) for o in range(far_ops)],
        axis=0,
    ).astype(jnp.bfloat16)
    own_term, highs, lows, far_rows = [], [], [], []
    for s in range(species):
        nearby = jnp.concatenate(
            [x.astype(jnp.float32) for x in (before[s], ghosts[0, s], ghosts[1, s], after[s])],
            axis=0,
        ).astype(jnp.bfloat16)
        grouped = jnp.dot(weights, nearby, preferred_element_type=jnp.float32)
        own_term.append(grouped[:slots])
        high, low = split(grouped[slots:])
        highs.append(high)
        lows.append(low)
        source = jnp.concatenate(
            [everyone[e, s * leaf_dev : (s + 1) * leaf_dev, :] for e in range(n)], axis=0
        )
        far_rows.append(
            jnp.dot(picks, source, preferred_element_type=jnp.float32)
        )
    total = jnp.concatenate(own_term, axis=0)
    for o in range(near_ops):
        part = slice(o * slots, (o + 1) * slots)
        stacked = jnp.concatenate(
            [x[part].astype(jnp.float32) for x in highs + lows], axis=0
        ).astype(jnp.bfloat16)
        product = jnp.dot(stacked, near_mat[o], preferred_element_type=jnp.float32)
        total = total + (product[: species * slots] + product[species * slots :])
    expansion = jnp.zeros((species * slots, trans.shape[2]), jnp.float32)
    for o in range(far_ops):
        rows_o = jnp.concatenate(
            [x[o * slots : (o + 1) * slots] for x in far_rows], axis=0
        ).astype(jnp.bfloat16)
        expansion = expansion + jnp.dot(rows_o, trans[o], preferred_element_type=jnp.float32)
    total = total + jnp.dot(
        expansion.astype(jnp.bfloat16), down[...], preferred_element_type=jnp.float32
    )
    for s in range(species):
        out[s] = jnp.where(live, total[s * slots : (s + 1) * slots], 0.0)


def shards(
    coeffs, points, owner_leaf, reaction, fit_matrix, new_seg, near_src, near_op,
    near_mat, up_mat, far_src, trans_mat, down_mat,
):
    species, leaf_dev, width = coeffs.shape
    n = lax.axis_size("seg")
    blocks = owner_leaf.shape[1]
    count = leaf_dev * blocks
    padded_width = -(-width // 128) * 128
    slots = leaf_dev + 2 * MOVE
    table = jnp.concatenate([new_seg[:, None], near_src, near_op, far_src], axis=1)
    table = jnp.pad(table, ((MOVE, MOVE), (0, 0)), constant_values=-1)
    mine = jnp.transpose(coeffs, (1, 0, 2))
    everyone = pair_gather(mine, "seg", 0).reshape(n * leaf_dev, species, width)
    values = pl.pallas_call(
        evaluate_kernel,
        out_shape=jax.ShapeDtypeStruct((species, count, PB), jnp.float32),
        in_specs=[SMEM, VMEM, VMEM],
        out_specs=VMEM,
        scratch_shapes=[
            pltpu.VMEM((8, padded_width), jnp.float32),
            pltpu.VMEM((count * species * ROWS, 128), jnp.float32),
            pltpu.VMEM((3, 16 * count, PB), jnp.float32),
        ],
        compiler_params=pltpu.CompilerParams(vmem_limit_bytes=LIMIT),
        name="evaluate",
    )(owner_leaf, everyone, points)
    gathered = pair_gather(values, "sp", 1)
    half = leaf_dev // 2
    ghosts, equivalent = pl.pallas_call(
        refit_kernel,
        out_shape=(
            jax.ShapeDtypeStruct((2, species, half, width), jnp.bfloat16),
            jax.ShapeDtypeStruct((species * leaf_dev, up_mat.shape[1]), jnp.bfloat16),
        ),
        in_specs=[SMEM, VMEM, VMEM, VMEM, VMEM],
        out_specs=(VMEM, VMEM),
        scratch_shapes=[pltpu.VMEM((species * leaf_dev, blocks * PB), jnp.float32)],
        compiler_params=pltpu.CompilerParams(vmem_limit_bytes=LIMIT),
        name="refit",
    )(reaction, values, gathered, fit_matrix, up_mat)
    before, after, all_equivalent = pl.pallas_call(
        functools.partial(exchange_kernel, n),
        out_shape=(
            jax.ShapeDtypeStruct((species, half, width), jnp.bfloat16),
            jax.ShapeDtypeStruct((species, half, width), jnp.bfloat16),
            jax.ShapeDtypeStruct((n,) + equivalent.shape, jnp.bfloat16),
        ),
        in_specs=[ANY, ANY],
        out_specs=(ANY, ANY, ANY),
        scratch_shapes=[
            pltpu.SemaphoreType.DMA((n + 1,)),
            pltpu.SemaphoreType.DMA((n + 1,)),
            pltpu.SemaphoreType.DMA,
        ],
        compiler_params=pltpu.CompilerParams(collective_id=2, has_side_effects=True),
        name="exchange",
    )(ghosts, equivalent)
    return pl.pallas_call(
        functools.partial(
            finish_kernel, near_count=near_src.shape[1], far_count=far_src.shape[1]
        ),
        out_shape=jax.ShapeDtypeStruct((species, slots, width), jnp.float32),
        in_specs=[VMEM] * 8,
        out_specs=VMEM,
        compiler_params=pltpu.CompilerParams(vmem_limit_bytes=LIMIT),
        name="finish",
    )(table, ghosts, before, after, all_equivalent, near_mat, trans_mat, down_mat)


def solution(mesh):
    placed = (P("sp", "seg", None), P(None, "seg", None), P("seg", None)) + (P(),) * 10
    return jax.shard_map(
        shards, mesh=mesh, in_specs=placed, out_specs=P("sp", "seg", None), check_vma=False
    )
```

time: 236 us -> 68.8 us (0.29)
  local copies, waits for them, and re-layouts: 105 us -> 6.72 us
  Pallas kernels: 0 us -> 61.7 us
  matrix products: 41.4 us -> 0 us
  blocking collectives: 37.5 us -> 0 us
  waiting for transfers between devices: 27.6 us -> 0 us
  starting transfers between devices: 15.5 us -> 0 us
  other arithmetic: 6.43 us -> 0.01 us
    gather x21 -> x0, local copies, waits for them, and re-layouts: 77.8 us -> none  [the longest x12 65.1 us: evaluate(): dense_coef = jnp.take(padded, jnp.asarray(lookup), axis=-1)]
    pallas_call x0 -> x6, Pallas kernels: none -> 61.7 us  [the longest x2 26.3 us: pair_gather(): pl.pallas_call(functools.partial(pair_gather_kernel, axis, n), out_shape=...]
    dot_general x24 -> x0, matrix products: 41.4 us -> none  [the longest x6 20.5 us: evaluate(): jnp.einsum('sqk,kp->sqp', dense_coef, along_z, precision=precise)]
    all_gather x2 -> x0, blocking collectives: 37.5 us -> none  [the longest x1 30.7 us: shards(): block_piece = lax.all_gather(equivalent, 'seg', axis=1, tiled=True)]
    all_to_all x2 -> x0, waiting for transfers between devices: 27.6 us -> none  [the longest x1 22.1 us: shards(): lax.all_to_all(picked.reshape(sources, item_count, local_species, coef_wi...]
    all_to_all x2 -> x0, starting transfers between devices: 11 us -> none  [the longest x1 7.31 us: shards(): lax.all_to_all(slot_leaf.reshape(segments, capacity), 'seg', split_axis=0...]
    dynamic_slice x12 -> x0, local copies, waits for them, and re-layouts: 10.8 us -> none  [evaluate_many(): lax.map(lambda block_args: evaluate(block_args[0], block_args[1]), (coef_...]
    ppermute x2 -> x0, starting transfers between devices: 4.44 us -> none  [the longest x1 3.15 us: extended(): before = lax.ppermute(last, axis, up)]
  transfers between devices with their start and end apart: 4 -> 0, of which waited for: 2 -> 0; matrix products, arithmetic and copies ran while one was open for 4% -> 0% of each run, Pallas kernels for 0% -> 0%
where the time goes in v1:
time: 68.8 us; the launch traced here: 68.5 us
  Pallas kernels  61.7 us (90%)
  local copies, waits for them, and re-layouts  6.72 us (10%)
    pallas_call x2, Pallas kernels, pair_gather(): pl.pallas_call(functools.partial(pair_gather_kernel, axis, n), out_shape=...  26.3 us
    pallas_call x1, Pallas kernels, shards(): pl.pallas_call(evaluate_kernel, out_shape=jax.ShapeDtypeStruct((species,...  19.8 us
    pallas_call x1, Pallas kernels, shards(): pl.pallas_call(functools.partial(exchange_kernel, n), out_shape=(jax.Shap...  8.76 us
    unnamed x16, local copies, waits for them, and re-layouts  5.99 us
    pallas_call x1, Pallas kernels, shards(): pl.pallas_call(functools.partial(finish_kernel, near_count=near_src.shape...  3.69 us
    pallas_call x1, Pallas kernels, shards(): pl.pallas_call(refit_kernel, out_shape=(jax.ShapeDtypeStruct((2, species,...  3.15 us

profile of v1, /device:TPU:0, one launch (start us, length us, event | category | flops | bytes accessed | tf_op | source)
XLA Modules:
  0.0 68.5 jit_solution(17235920225296825662)
XLA Ops:
  0.0 0.0 copy-start
  0.0 1.8 %copy.28 = f32[2,16,680]{2,0,1:T(2,128)} copy(f32[2,16,680]{2,1,0:T(8,128)} %param.13) | data formatting | bytes 174080 | tf_op args[0]
  1.8 19.7 %gather_seg.1 = f32[8,16,2,680]{3,2,1,0:T(2,128)} custom-call(f32[16,2,680]{2,1,0:T(2,128)} %bitcast.6), custom_call_target="tpu_custom_call" | custom-call | tf_op jit(solution)/shard_map/gather_seg/pallas_call | solution.py:80
  21.5 1.4 %copy.24.owner = s32[16,6]{1,0:T(8,128)} copy(s32[16,6]{0,1:T(8,128)} %param.15) | data formatting | bytes 768 | tf_op args[2]
  22.8 19.8 %evaluate.1.src.own = f32[2,96,128]{2,1,0:T(8,128)} custom-call(s32[16,6]{1,0:T(8,128)} %copy.24.owner, f32[128,2,680]{2,1,0:T(2,128)} %bitcast.5, f32[3,16,768]{2,1,0:T(8,128)} %points.1), custom_call_target="tpu_custom_call" | custom-call | tf_op jit(solution)/shard_map/evaluate/pallas_call | solution.py:340
  42.6 6.6 %gather_sp.1.gathered = f32[4,2,96,128]{3,2,1,0:T(8,128)} custom-call(f32[2,96,128]{2,1,0:T(8,128)} %evaluate.1.src.own), custom_call_target="tpu_custom_call" | custom-call | tf_op jit(solution)/shard_map/gather_sp/pallas_call | solution.py:80
  49.3 0.0 copy-done
  49.3 0.0 copy-start.1
  49.3 1.9 %copy.25.fit = f32[768,680]{1,0:T(8,128)} copy(f32[768,680]{0,1:T(8,128)S(1)} %copy-done) | data formatting | bytes 4177920 | tf_op args[4]
  51.2 0.0 copy-done.1
  51.2 0.0 copy-start.2
  51.2 0.0 copy-start.3
  51.2 0.0 copy-start.4
  51.2 0.0 copy-start.5
  51.2 0.9 %copy.26.up = bf16[680,152]{1,0:T(8,128)(2,1)} copy(bf16[680,152]{0,1:T(8,128)(2,1)S(1)} %copy-done.1) | data formatting | bytes 413440 | tf_op args[9]
  52.2 3.2 %refit.1 = (bf16[2,2,8,680]{3,2,1,0:T(8,128)(2,1)}, bf16[32,152]{1,0:T(8,128)(2,1)}) custom-call(f32[8,8]{1,0:T(8,128)} %reaction.1, f32[2,96,128]{2,1,0:T(8,128)} %evaluate.1.src.own, f32[4,2,96,128]{3,2,1,0:T(8,128)} %gather_sp.1.gathered, f32[768,680]{1,0:T(8,128)} %copy.25.fit, bf16[680,152]{1,0:T(8,128)(2,1)} %copy.26.up), custom_call_target="tpu_custom_call" | custom-call | tf_op jit(solution)/shard_map/refit/pallas_call | solution.py:355
  55.3 8.8 %exchange.1 = (bf16[2,8,680]{2,1,0:T(8,128)(2,1)}, bf16[2,8,680]{2,1,0:T(8,128)(2,1)}, bf16[8,32,152]{2,1,0:T(8,128)(2,1)}) custom-call(bf16[2,2,8,680]{3,2,1,0:T(8,128)(2,1)} %get-tuple-element.10.ghosts, bf16[32,152]{1,0:T(8,128)(2,1)} %get-tuple-element.11.equivalent), custom_call_target="tpu_custom_call" | custom-call | tf_op jit(solution)/shard_map/exchange/pallas_call | solution.py:367
  64.1 0.0 copy-done.2
  64.1 0.0 copy-done.3
  64.1 0.0 copy-done.4
  64.1 0.0 copy-done.5
  64.1 0.1 copy.22
  64.2 0.6 pad.4.table
  64.9 3.7 %finish.1 = f32[2,24,680]{2,1,0:T(8,128)} custom-call(s32[136,41]{1,0:T(8,128)} %pad.4.table, bf16[2,2,8,680]{3,2,1,0:T(8,128)(2,1)} %get-tuple-element.10.ghosts, bf16[2,8,680]{2,1,0:T(8,128)(2,1)} %get-tuple-element.12.before, bf16[2,8,680]{2,1,0:T(8,128)(2,1)} %get-tuple-element.13.after, bf16[8,32,152]{2,1,0:T(8,128)(2,1)} %get-tuple-element.14.everyone, ...), custom_call_target="tpu_custom_call" | custom-call | tf_op jit(solution)/shard_map/finish/pallas_call | solution.py:384
  (1 shorter events, 0.0 us)
Async XLA Ops:
  0.0 49.3 %copy-start = (f32[768,680]{0,1:T(8,128)S(1)}, f32[768,680]{0,1:T(8,128)}, u32[]{:S(2)}) copy-start(f32[768,680]{0,1:T(8,128)} %param.17) | copy-start | bytes 6266884
  49.3 2.0 %copy-start.1 = (bf16[680,152]{0,1:T(8,128)(2,1)S(1)}, bf16[680,152]{0,1:T(8,128)(2,1)}, u32[]{:S(2)}) copy-start(bf16[680,152]{0,1:T(8,128)(2,1)} %param.22) | copy-start | bytes 620164
  51.2 12.8 %copy-start.2 = (s32[128,16]{0,1:T(8,128)S(1)}, s32[128,16]{0,1:T(8,128)}, u32[]{:S(2)}) copy-start(s32[128,16]{0,1:T(8,128)} %param.20) | copy-start | bytes 24580
  51.2 12.9 %copy-start.3 = (s32[128,16]{0,1:T(8,128)S(1)}, s32[128,16]{0,1:T(8,128)}, u32[]{:S(2)}) copy-start(s32[128,16]{0,1:T(8,128)} %param.19) | copy-start | bytes 24580
  51.2 12.9 %copy-start.4 = (s32[128,8]{0,1:T(8,128)S(1)}, s32[128,8]{0,1:T(8,128)}, u32[]{:S(2)}) copy-start(s32[128,8]{0,1:T(8,128)} %param.23) | copy-start | bytes 12292
  51.2 12.9 %copy-start.5 = (s32[128]{0:T(128)S(1)}, s32[128]{0:T(128)}, u32[]{:S(2)}) copy-start(s32[128]{0:T(128)} %param.18) | copy-start | bytes 1540

commit v2 on v1

--- a/solution.py
+++ b/solution.py
@@ -323,6 +323,376 @@
         out[s] = jnp.where(live, total[s * slots : (s + 1) * slots], 0.0)
 
 
+def step_kernel(
+    n, n_sp, pieces, near_count, far_count,
+    coeffs, points_in, owner_in, reaction_in, fit_in, table_in, near_in, up_in, trans_in, down_in,
+    out,
+    slots, points, owner, reaction, fit, table, near_mat, up, trans, down,
+    dense, cheb, fit_high, fit_low, gathered, ghosts, before, after, everyone, weights, picks,
+    local, send, recv, sp_send, sp_recv, ex_send, ex_recv,
+):
+    species, leaf_dev, width = coeffs.shape
+    blocks = owner.shape[1]
+    count = leaf_dev * blocks
+    starts, _ = run_starts()
+    me = lax.axis_index("seg")
+    me_sp = lax.axis_index("sp")
+    half = n // 2
+    partner = me + 1 - 2 * lax.rem(me, 2)
+    ahead = [lax.rem(me + p, n) for p in range(n)]
+    behind = [lax.rem(me + n - p, n) for p in range(n)]
+    sp_ahead = [lax.rem(me_sp + p, n_sp) for p in range(n_sp)]
+    sp_behind = [lax.rem(me_sp + n_sp - p, n_sp) for p in range(n_sp)]
+
+    moves = [
+        (coeffs, slots.at[me]), (points_in, points), (owner_in, owner), (reaction_in, reaction),
+        (fit_in, fit), (table_in, table), (near_in, near_mat), (up_in, up), (trans_in, trans),
+        (down_in, down),
+    ]
+    loads = [pltpu.make_async_copy(a, b, local.at[k]) for k, (a, b) in enumerate(moves)]
+    for load in loads:
+        load.start()
+
+    barrier = pltpu.get_barrier_semaphore()
+    for to in ahead[1:]:
+        pl.semaphore_signal(barrier, inc=1, device_id={"seg": to}, device_id_type=MESH)
+    for to in sp_ahead[1:]:
+        pl.semaphore_signal(barrier, inc=1, device_id={"sp": to}, device_id_type=MESH)
+    pl.semaphore_wait(barrier, n + n_sp - 2)
+
+    copies = []
+    for p in range(1, half):
+        copies.append(remote(coeffs, slots.at[me], send.at[p], recv.at[p], "seg", ahead[2 * p]))
+        copies[-1].start()
+    copies.append(remote(coeffs, slots.at[me], send.at[half], recv.at[half], "seg", partner))
+    copies[-1].start()
+
+    loads[1].wait()
+    for axis in range(3):
+        for m in range(blocks):
+            for h in range(leaf_dev // 8):
+                x = points[axis, 8 * h : 8 * h + 8, PB * m : PB * m + PB]
+                first = 16 * (m * leaf_dev + 8 * h)
+                prior, here = jnp.ones_like(x), x
+                cheb[axis, pl.ds(first, 8, stride=16), :] = prior
+                for d in range(1, ORDER + 1):
+                    cheb[axis, pl.ds(first + d, 8, stride=16), :] = here
+                    prior, here = here, 2.0 * x * here - prior
+                cheb[axis, pl.ds(first + ORDER + 1, 8, stride=16), :] = jnp.zeros_like(x)
+
+    lane = lax.broadcasted_iota(jnp.int32, (8, 128), 1)
+    zero = jnp.zeros((8, 128), jnp.float32)
+    full = width // 128
+    flat = dense.reshape(n * leaf_dev * species * ROWS, 128)
+
+    def expand(slot):
+        def chunk(c, carry):
+            s = lax.div(c, leaf_dev // 8)
+            h = lax.rem(c, leaf_dev // 8)
+            part_rows = pl.ds(pl.multiple_of(8 * h, 8), 8)
+            tiles = []
+            for t in range(full + (width % 128 > 0)):
+                if t < full:
+                    x = slots[slot, s, part_rows, 128 * t : 128 * t + 128]
+                else:
+                    x = slots[slot, s, part_rows, 128 * t : width]
+                    x = jnp.concatenate(
+                        [x, jnp.zeros((8, 128 - width % 128), jnp.float32)], axis=1
+                    )
+                x_high = x.astype(jnp.bfloat16).astype(jnp.float32)
+                tiles.append((x_high, x - x_high))
+            base = ((slot * leaf_dev + 8 * h) * species + s) * ROWS
+            for g, (i, upper) in enumerate(GROUPS):
+                for k in range(8):
+                    j = 8 * upper + k
+                    if i + j > ORDER:
+                        piece = zero
+                    else:
+                        length = ORDER + 1 - i - j
+                        t, shift = divmod(starts[i, j], 128)
+                        parts = []
+                        for kind in range(2):
+                            turn = (128 - shift + 16 * kind) % 128
+                            part = tiles[t][kind]
+                            if turn:
+                                part = pltpu.roll(part, turn, 1)
+                            if shift + length > 128:
+                                rest = pltpu.roll(tiles[t + 1][kind], turn, 1)
+                                part = jnp.where(lane < 128 - shift + 16 * kind, part, rest)
+                            parts.append(part)
+                        second = jnp.where((lane >= 16) & (lane < 16 + length), parts[1], zero)
+                        piece = jnp.where(lane < length, parts[0], second)
+                    flat[pl.ds(base + 8 * g + k, 8, stride=species * ROWS), :] = piece
+            return carry
+
+        lax.fori_loop(0, species * leaf_dev // 8, chunk, 0)
+
+    loads[0].wait()
+
+    def arrive(p, carry):
+        slot = lax.rem(me + n - 2 * p, n)
+        other = lax.rem(partner + n - 2 * p, n)
+
+        @pl.when(p > 0)
+        def _():
+            here = slots.at[slot]
+            remote(here, here, send.at[p], recv.at[p], "seg", partner).wait_recv()
+            remote(here, here, send.at[half + p], recv.at[half + p], "seg", partner).start()
+
+        expand(slot)
+        there = slots.at[other]
+        remote(there, there, send.at[half + p], recv.at[half + p], "seg", partner).wait_recv()
+        expand(other)
+
+        @pl.when(p == 0)
+        def _():
+            local_tables()
+
+        return carry
+
+    def local_tables():
+        loads[4].wait()
+        for k in range(0, fit.shape[0], PB):
+            high, low = split(fit[k : k + PB])
+            fit_high[k : k + PB] = high
+            fit_low[k : k + PB] = low
+        loads[5].wait()
+        slot_count = out.shape[1]
+        rows = table[pl.ds(pl.multiple_of(me * leaf_dev, 8), slot_count), :]
+        live = rows[:, 0:1] == me
+        margin = MOVE + REACH
+        base = me * leaf_dev - margin
+        seen = leaf_dev + 2 * margin
+        near_lane = lax.broadcasted_iota(jnp.int32, (slot_count, seen), 1)
+        slot_row = lax.broadcasted_iota(jnp.int32, (slot_count, seen), 0)
+        near_from = rows[:, 1 : 1 + near_count]
+        near_kind = rows[:, 1 + near_count : 1 + 2 * near_count]
+        far_from = rows[:, 1 + 2 * near_count : 1 + 2 * near_count + far_count]
+        near_from = jnp.where(live & (near_from >= 0), near_from - base, -1)
+        far_from = jnp.where(live & (far_from >= 0), far_from, -1)
+        found = [((near_lane == slot_row + REACH) & live).astype(jnp.float32)]
+        found += [jnp.zeros((slot_count, seen), jnp.float32) for _ in range(near_mat.shape[0])]
+        for q in range(near_count):
+            hit = near_lane == near_from[:, q : q + 1]
+            for o in range(near_mat.shape[0]):
+                chosen = hit & (near_kind[:, q : q + 1] == o)
+                found[1 + o] = found[1 + o] + chosen.astype(jnp.float32)
+        weights[...] = jnp.concatenate(found, axis=0).astype(jnp.bfloat16)
+        far_lane = lax.broadcasted_iota(jnp.int32, (slot_count, n * leaf_dev), 1)
+        picks[...] = jnp.concatenate(
+            [(far_lane == far_from[:, o : o + 1]).astype(jnp.float32) for o in range(far_count)],
+            axis=0,
+        ).astype(jnp.bfloat16)
+
+    lax.fori_loop(0, half, arrive, 0)
+
+    loads[2].wait()
+
+    def block(b):
+        leaf = owner[lax.rem(b, leaf_dev), lax.div(b, leaf_dev)]
+        lhs = dense[leaf][:, 0:32].astype(jnp.bfloat16)
+        here = pl.ds(pl.multiple_of(b * 16, 16), 16)
+        tx, ty, tz = cheb[0, here, :], cheb[1, here, :], cheb[2, here, :]
+        tz_high = tz.astype(jnp.bfloat16).astype(jnp.float32)
+        rhs = jnp.concatenate(
+            [
+                jnp.concatenate([tz_high, tz - tz_high], axis=1),
+                jnp.concatenate([tz_high, jnp.zeros_like(tz)], axis=1),
+            ],
+            axis=0,
+        ).astype(jnp.bfloat16)
+        both = jnp.dot(lhs, rhs, preferred_element_type=jnp.float32)
+        inner = both[:, :PB] + both[:, PB:]
+        for s in range(species):
+            total = [None, None]
+            for g, (i, upper) in enumerate(GROUPS):
+                r = s * ROWS + 8 * g
+                term = inner[r : r + 8] * tx[i : i + 1]
+                total[upper] = term if total[upper] is None else total[upper] + term
+            summed = total[0] * ty[0:8] + total[1] * ty[8:16]
+            gathered[me_sp, s, pl.ds(b, 1), :] = jnp.sum(summed, axis=0, keepdims=True)
+
+    step = count // pieces
+
+    def part_of(slot, k):
+        return gathered.at[slot, :, step * k : step * (k + 1), :]
+
+    for k in range(pieces):
+
+        def several(c, carry, k=k):
+            for u in range(4):
+                block(step * k + 4 * c + u)
+            return carry
+
+        lax.fori_loop(0, step // 4, several, 0)
+        mine = part_of(me_sp, k)
+        for p in range(1, n_sp):
+            copies.append(
+                remote(mine, mine, sp_send.at[k, p], sp_recv.at[k, p], "sp", sp_ahead[p])
+            )
+            copies[-1].start()
+
+    loads[3].wait()
+    rows_total = species * leaf_dev
+    refitted = jnp.zeros((rows_total, width), jnp.float32)
+    per = step // leaf_dev
+    for k in range(pieces):
+        for p in range(1, n_sp):
+            there = part_of(sp_behind[p], k)
+            remote(there, there, sp_send.at[k, p], sp_recv.at[k, p], "sp", sp_ahead[p]).wait_recv()
+        by_species = []
+        for s in range(species):
+            mixing = jnp.zeros((step, PB), jnp.float32)
+            for r in range(n_sp * species):
+                other = gathered[r // species, r % species, step * k : step * (k + 1), :]
+                mixing = mixing + reaction[me_sp * species + s, r] * other
+            by_species.append(
+                gathered[me_sp, s, step * k : step * (k + 1), :] + jnp.tanh(mixing)
+            )
+        reacted = jnp.concatenate(
+            [
+                jnp.concatenate(
+                    [x[m * leaf_dev : (m + 1) * leaf_dev] for x in by_species], axis=0
+                )
+                for m in range(per)
+            ],
+            axis=1,
+        )
+        high, low = split(reacted)
+        nodes = slice(k * per * PB, (k + 1) * per * PB)
+        main = jnp.dot(
+            jnp.concatenate([high, low], axis=0), fit_high[nodes],
+            preferred_element_type=jnp.float32,
+        )
+        rest = jnp.dot(high, fit_low[nodes], preferred_element_type=jnp.float32)
+        refitted = refitted + (main[:rows_total] + (main[rows_total:] + rest))
+    rounded = refitted.astype(jnp.bfloat16)
+    half_leaf = leaf_dev // 2
+    for s in range(species):
+        for h in range(2):
+            first = s * leaf_dev + h * half_leaf
+            ghosts[h, s] = refitted[first : first + half_leaf].astype(jnp.bfloat16)
+    rise = remote(ghosts.at[1], before, ex_send.at[0], ex_recv.at[0], "seg", ahead[1])
+    fall = remote(ghosts.at[0], after, ex_send.at[n], ex_recv.at[n], "seg", behind[1])
+    loads[7].wait()
+    everyone[me] = jnp.dot(
+        rounded, up[...], preferred_element_type=jnp.float32
+    ).astype(jnp.bfloat16)
+    for p in range(1, n):
+        mine = everyone.at[me]
+        copies.append(remote(mine, mine, ex_send.at[p], ex_recv.at[p], "seg", ahead[p]))
+        copies[-1].start()
+    rise.start()
+    fall.start()
+
+    near_ops, far_ops = near_mat.shape[0], trans.shape[0]
+    slot_count = out.shape[1]
+    loads[6].wait()
+    loads[8].wait()
+    loads[9].wait()
+    rise.wait()
+    fall.wait()
+    own_term, highs, lows = [], [], []
+    for s in range(species):
+        nearby = jnp.concatenate(
+            [x.astype(jnp.float32) for x in (before[s], ghosts[0, s], ghosts[1, s], after[s])],
+            axis=0,
+        ).astype(jnp.bfloat16)
+        grouped = jnp.dot(weights[...], nearby, preferred_element_type=jnp.float32)
+        own_term.append(grouped[:slot_count])
+        high, low = split(grouped[slot_count:])
+        highs.append(high)
+        lows.append(low)
+    total = jnp.concatenate(own_term, axis=0)
+    for o in range(near_ops):
+        part = slice(o * slot_count, (o + 1) * slot_count)
+        stacked = jnp.concatenate(
+            [x[part].astype(jnp.float32) for x in highs + lows], axis=0
+        ).astype(jnp.bfloat16)
+        product = jnp.dot(stacked, near_mat[o], preferred_element_type=jnp.float32)
+        total = total + (product[: species * slot_count] + product[species * slot_count :])
+    for p in range(1, n):
+        there = everyone.at[behind[p]]
+        remote(there, there, ex_send.at[p], ex_recv.at[p], "seg", ahead[p]).wait_recv()
+    far_rows = []
+    for s in range(species):
+        source = jnp.concatenate(
+            [everyone[e, s * leaf_dev : (s + 1) * leaf_dev, :] for e in range(n)], axis=0
+        )
+        far_rows.append(jnp.dot(picks[...], source, preferred_element_type=jnp.float32))
+    expansion = jnp.zeros((species * slot_count, trans.shape[2]), jnp.float32)
+    for o in range(far_ops):
+        rows_o = jnp.concatenate(
+            [x[o * slot_count : (o + 1) * slot_count] for x in far_rows], axis=0
+        ).astype(jnp.bfloat16)
+        expansion = expansion + jnp.dot(rows_o, trans[o], preferred_element_type=jnp.float32)
+    total = total + jnp.dot(
+        expansion.astype(jnp.bfloat16), down[...], preferred_element_type=jnp.float32
+    )
+    live = table[pl.ds(pl.multiple_of(me * leaf_dev, 8), slot_count), 0:1] == me
+    for s in range(species):
+        out[s] = jnp.where(live, total[s * slot_count : (s + 1) * slot_count], 0.0)
+    for copy in copies:
+        copy.wait_send()
+    for p in range(1, half):
+        there = slots.at[behind[2 * p]]
+        remote(there, there, send.at[half + p], recv.at[half + p], "seg", partner).wait_send()
+
+
+def whole_step(
+    coeffs, points, owner_leaf, reaction, fit_matrix, table, near_mat, up_mat, trans_mat,
+    down_mat, near_count, far_count,
+):
+    species, leaf_dev, width = coeffs.shape
+    n, n_sp = lax.axis_size("seg"), lax.axis_size("sp")
+    blocks = owner_leaf.shape[1]
+    count = leaf_dev * blocks
+    slots = leaf_dev + 2 * MOVE
+    seen = leaf_dev + 2 * (MOVE + REACH)
+    half = leaf_dev // 2
+    pieces = 3
+    f32, bf16, i32 = jnp.float32, jnp.bfloat16, jnp.int32
+    dma = pltpu.SemaphoreType.DMA
+    return pl.pallas_call(
+        functools.partial(step_kernel, n, n_sp, pieces, near_count, far_count),
+        out_shape=jax.ShapeDtypeStruct((species, slots, width), f32),
+        in_specs=[ANY] * 10,
+        out_specs=VMEM,
+        scratch_shapes=[
+            pltpu.VMEM((n,) + coeffs.shape, f32),
+            pltpu.VMEM(points.shape, f32),
+            pltpu.SMEM(owner_leaf.shape, i32),
+            pltpu.SMEM(reaction.shape, f32),
+            pltpu.VMEM(fit_matrix.shape, f32),
+            pltpu.VMEM(table.shape, i32),
+            pltpu.VMEM(near_mat.shape, bf16),
+            pltpu.VMEM(up_mat.shape, bf16),
+            pltpu.VMEM(trans_mat.shape, bf16),
+            pltpu.VMEM(down_mat.shape, bf16),
+            pltpu.VMEM((n * leaf_dev, species * ROWS, 128), f32),
+            pltpu.VMEM((3, 16 * count, PB), f32),
+            pltpu.VMEM(fit_matrix.shape, bf16),
+            pltpu.VMEM(fit_matrix.shape, bf16),
+            pltpu.VMEM((n_sp, species, count, PB), f32),
+            pltpu.VMEM((2, species, half, width), bf16),
+            pltpu.VMEM((species, half, width), bf16),
+            pltpu.VMEM((species, half, width), bf16),
+            pltpu.VMEM((n, species * leaf_dev, up_mat.shape[1]), bf16),
+            pltpu.VMEM(((1 + near_mat.shape[0]) * slots, seen), bf16),
+            pltpu.VMEM((far_count * slots, n * leaf_dev), bf16),
+            dma((10,)), dma((n,)), dma((n,)), dma((pieces, n_sp)), dma((pieces, n_sp)),
+            dma((n + 1,)), dma((n + 1,)),
+        ],
+        compiler_params=pltpu.CompilerParams(
+            collective_id=3, has_side_effects=True, vmem_limit_bytes=LIMIT
+        ),
+        name="step",
+    )(
+        coeffs, points, owner_leaf, reaction, fit_matrix, table, near_mat, up_mat, trans_mat,
+        down_mat,
+    )
+
+
 def shards(
     coeffs, points, owner_leaf, reaction, fit_matrix, new_seg, near_src, near_op,
     near_mat, up_mat, far_src, trans_mat, down_mat,
@@ -335,6 +705,11 @@
     slots = leaf_dev + 2 * MOVE
     table = jnp.concatenate([new_seg[:, None], near_src, near_op, far_src], axis=1)
     table = jnp.pad(table, ((MOVE, MOVE), (0, 0)), constant_values=-1)
+    if n * leaf_dev * species * ROWS * 512 <= LIMIT // 2:
+        return whole_step(
+            coeffs, points, owner_leaf, reaction, fit_matrix, table, near_mat, up_mat,
+            trans_mat, down_mat, near_src.shape[1], far_src.shape[1],
+        )
     mine = jnp.transpose(coeffs, (1, 0, 2))
     everyone = pair_gather(mine, "seg", 0).reshape(n * leaf_dev, species, width)
     values = pl.pallas_call(

time: 68.8 us -> 59.9 us (0.87)
  Pallas kernels: 61.7 us -> 50.4 us
  local copies, waits for them, and re-layouts: 6.72 us -> 8.55 us
  other arithmetic: 0.01 us -> 0.74 us
    pallas_call x6 -> x1, Pallas kernels: 61.7 us -> 50.4 us  [whole_step(): pl.pallas_call(functools.partial(step_kernel, n, n_sp, pieces, near_count...]
    unnamed x16 -> x4, local copies, waits for them, and re-layouts: 5.99 us -> 7.8 us
    concatenate x1, other arithmetic: 0.01 us -> 0.74 us  [shards(): jnp.concatenate([new_seg[:, None], near_src, near_op, far_src], axis=1)]
where the time goes in v2:
time: 59.9 us; the launch traced here: 59.7 us
  Pallas kernels  50.4 us (84%)
  local copies, waits for them, and re-layouts  8.55 us (14%)
  other arithmetic  0.74 us (1%)
    pallas_call x1, Pallas kernels, whole_step(): pl.pallas_call(functools.partial(step_kernel, n, n_sp, pieces, near_count...  50.4 us
    unnamed x4, local copies, waits for them, and re-layouts  7.8 us

profile of v2, /device:TPU:0, one launch (start us, length us, event | category | flops | bytes accessed | tf_op | source)
XLA Modules:
  0.0 59.7 jit_solution(4392072374746998763)
XLA Ops:
  0.0 1.4 %copy.22.owner_in = s32[16,6]{1,0:T(8,128)} copy(s32[16,6]{0,1:T(8,128)} %param.15) | data formatting | bytes 768 | tf_op args[2]
  1.4 0.7 %pad_add_fusion = s32[128,41]{0,1:T(8,128)S(1)} fusion(s32[128,8]{0,1:T(8,128)} %param.23, s32[128,16]{0,1:T(8,128)} %param.20, s32[128,16]{0,1:T(8,128)} %param.19, s32[128,1]{0,1:T(1,128)} %bitcast.1), kind=kLoop, calls=%fused_computation | loop fusion | flops 15744 | bytes 41984 | tf_op jit(solution)/shard_map/concatenate | solution.py:706
  2.1 0.1 copy.21
  2.2 0.6 %pad.4.table_in = s32[136,41]{1,0:T(8,128)} pad(s32[128,41]{1,0:T(8,128)S(1)} %copy.21, s32[]{:T(128)} %constant.0.clone.1), padding=4_4x0_0 | pad | bytes 43300 | tf_op jit(solution)/shard_map/jit(_pad)/pad | solution.py:707
  2.8 1.8 %copy.24.up_in = bf16[680,152]{1,0:T(8,128)(2,1)} copy(bf16[680,152]{0,1:T(8,128)(2,1)} %param.22) | data formatting | bytes 413440 | tf_op args[9]
  4.7 3.0 %copy.23.fit_in = f32[768,680]{1,0:T(8,128)} copy(f32[768,680]{0,1:T(8,128)} %param.17) | data formatting | bytes 4177920 | tf_op args[4]
  7.7 50.4 %step.1 = f32[2,24,680]{2,1,0:T(8,128)} custom-call(f32[2,16,680]{2,1,0:T(8,128)} %coeffs.1, f32[3,16,768]{2,1,0:T(8,128)} %points_in.1, s32[16,6]{1,0:T(8,128)} %copy.22.owner_in, f32[8,8]{1,0:T(8,128)} %reaction_in.1, f32[768,680]{1,0:T(8,128)} %copy.23.fit_in, s32[136,41]{1,0:T(8,128)} %pad.4.table_in, bf16[2,680,680]{2,1,0:T(8,128)(2,1)} %near_in.1, ...), custom_call_target="tpu_custom_call" | custom-call | tf_op jit(solution)/shard_map/step/pallas_call | solution.py:656
  58.1 1.6 %copy.26 = f32[2,24,680]{2,1,0:T(8,128)} copy(f32[2,24,680]{2,1,0:T(8,128)} %step.1) | data formatting | bytes 261120

commit v3 on v2

--- a/solution.py
+++ b/solution.py
@@ -323,6 +323,12 @@
         out[s] = jnp.where(live, total[s * slots : (s + 1) * slots], 0.0)
 
 
+def last_dims(x, y):
+    return lax.dot_general(
+        x, y, (((1,), (1,)), ((), ())), preferred_element_type=jnp.float32
+    )
+
+
 def step_kernel(
     n, n_sp, pieces, near_count, far_count,
     coeffs, points_in, owner_in, reaction_in, fit_in, table_in, near_in, up_in, trans_in, down_in,
@@ -332,7 +338,7 @@
     local, send, recv, sp_send, sp_recv, ex_send, ex_recv,
 ):
     species, leaf_dev, width = coeffs.shape
-    blocks = owner.shape[1]
+    blocks = owner.shape[0]
     count = leaf_dev * blocks
     starts, _ = run_starts()
     me = lax.axis_index("seg")
@@ -405,9 +411,7 @@
             for g, (i, upper) in enumerate(GROUPS):
                 for k in range(8):
                     j = 8 * upper + k
-                    if i + j > ORDER:
-                        piece = zero
-                    else:
+                    if i + j <= ORDER:
                         length = ORDER + 1 - i - j
                         t, shift = divmod(starts[i, j], 128)
                         parts = []
@@ -422,11 +426,20 @@
                             parts.append(part)
                         second = jnp.where((lane >= 16) & (lane < 16 + length), parts[1], zero)
                         piece = jnp.where(lane < length, parts[0], second)
-                    flat[pl.ds(base + 8 * g + k, 8, stride=species * ROWS), :] = piece
+                        flat[pl.ds(base + 8 * g + k, 8, stride=species * ROWS), :] = piece
             return carry
 
         lax.fori_loop(0, species * leaf_dev // 8, chunk, 0)
 
+    partial = [g for g, (i, upper) in enumerate(GROUPS) if i + 8 * upper + 7 > ORDER]
+
+    def clear(leaf, carry):
+        for s in range(species):
+            for g in partial:
+                dense[leaf, s * ROWS + 8 * g : s * ROWS + 8 * g + 8, :] = zero
+        return carry
+
+    lax.fori_loop(0, n * leaf_dev, clear, 0)
     loads[0].wait()
 
     def arrive(p, carry):
@@ -453,9 +466,9 @@
     def local_tables():
         loads[4].wait()
         for k in range(0, fit.shape[0], PB):
-            high, low = split(fit[k : k + PB])
-            fit_high[k : k + PB] = high
-            fit_low[k : k + PB] = low
+            high, low = split(fit[k : min(k + PB, width)])
+            fit_high[k : min(k + PB, width)] = high
+            fit_low[k : min(k + PB, width)] = low
         loads[5].wait()
         slot_count = out.shape[1]
         rows = table[pl.ds(pl.multiple_of(me * leaf_dev, 8), slot_count), :]
@@ -489,7 +502,7 @@
     loads[2].wait()
 
     def block(b):
-        leaf = owner[lax.rem(b, leaf_dev), lax.div(b, leaf_dev)]
+        leaf = owner[lax.div(b, leaf_dev), lax.rem(b, leaf_dev)]
         lhs = dense[leaf][:, 0:32].astype(jnp.bfloat16)
         here = pl.ds(pl.multiple_of(b * 16, 16), 16)
         tx, ty, tz = cheb[0, here, :], cheb[1, here, :], cheb[2, here, :]
@@ -560,11 +573,8 @@
         )
         high, low = split(reacted)
         nodes = slice(k * per * PB, (k + 1) * per * PB)
-        main = jnp.dot(
-            jnp.concatenate([high, low], axis=0), fit_high[nodes],
-            preferred_element_type=jnp.float32,
-        )
-        rest = jnp.dot(high, fit_low[nodes], preferred_element_type=jnp.float32)
+        main = last_dims(jnp.concatenate([high, low], axis=0), fit_high[:, nodes])
+        rest = last_dims(high, fit_low[:, nodes])
         refitted = refitted + (main[:rows_total] + (main[rows_total:] + rest))
     rounded = refitted.astype(jnp.bfloat16)
     half_leaf = leaf_dev // 2
@@ -575,9 +585,7 @@
     rise = remote(ghosts.at[1], before, ex_send.at[0], ex_recv.at[0], "seg", ahead[1])
     fall = remote(ghosts.at[0], after, ex_send.at[n], ex_recv.at[n], "seg", behind[1])
     loads[7].wait()
-    everyone[me] = jnp.dot(
-        rounded, up[...], preferred_element_type=jnp.float32
-    ).astype(jnp.bfloat16)
+    everyone[me] = last_dims(rounded, up[...]).astype(jnp.bfloat16)
     for p in range(1, n):
         mine = everyone.at[me]
         copies.append(remote(mine, mine, ex_send.at[p], ex_recv.at[p], "seg", ahead[p]))
@@ -645,7 +653,7 @@
 ):
     species, leaf_dev, width = coeffs.shape
     n, n_sp = lax.axis_size("seg"), lax.axis_size("sp")
-    blocks = owner_leaf.shape[1]
+    blocks = owner_leaf.shape[0]
     count = leaf_dev * blocks
     slots = leaf_dev + 2 * MOVE
     seen = leaf_dev + 2 * (MOVE + REACH)
@@ -677,7 +685,7 @@
             pltpu.VMEM((2, species, half, width), bf16),
             pltpu.VMEM((species, half, width), bf16),
             pltpu.VMEM((species, half, width), bf16),
-            pltpu.VMEM((n, species * leaf_dev, up_mat.shape[1]), bf16),
+            pltpu.VMEM((n, species * leaf_dev, up_mat.shape[0]), bf16),
             pltpu.VMEM(((1 + near_mat.shape[0]) * slots, seen), bf16),
             pltpu.VMEM((far_count * slots, n * leaf_dev), bf16),
             dma((10,)), dma((n,)), dma((n,)), dma((pieces, n_sp)), dma((pieces, n_sp)),
@@ -707,7 +715,7 @@
     table = jnp.pad(table, ((MOVE, MOVE), (0, 0)), constant_values=-1)
     if n * leaf_dev * species * ROWS * 512 <= LIMIT // 2:
         return whole_step(
-            coeffs, points, owner_leaf, reaction, fit_matrix, table, near_mat, up_mat,
+            coeffs, points, owner_leaf.T, reaction, fit_matrix.T, table, near_mat, up_mat.T,
             trans_mat, down_mat, near_src.shape[1], far_src.shape[1],
         )
     mine = jnp.transpose(coeffs, (1, 0, 2))

time: 59.9 us -> 51.6 us (0.86)
  local copies, waits for them, and re-layouts: 8.55 us -> 2.33 us
  Pallas kernels: 50.4 us -> 48.3 us
    unnamed x4 -> x1, local copies, waits for them, and re-layouts: 7.8 us -> 1.58 us
    pallas_call x1, Pallas kernels: 50.4 us -> 48.3 us  [whole_step(): pl.pallas_call(functools.partial(step_kernel, n, n_sp, pieces, near_count...]
where the time goes in v3:
time: 51.6 us; the launch traced here: 51.4 us
  Pallas kernels  48.3 us (94%)
  local copies, waits for them, and re-layouts  2.33 us (5%)
  other arithmetic  0.74 us (1%)
    pallas_call x1, Pallas kernels, whole_step(): pl.pallas_call(functools.partial(step_kernel, n, n_sp, pieces, near_count...  48.3 us
    unnamed x1, local copies, waits for them, and re-layouts  1.58 us

profile of v3, /device:TPU:0, one launch (start us, length us, event | category | flops | bytes accessed | tf_op | source)
XLA Modules:
  0.0 51.4 jit_solution(13341406987980815584)
XLA Ops:
  0.0 0.7 %pad_add_fusion = s32[128,41]{0,1:T(8,128)S(1)} fusion(s32[128,8]{0,1:T(8,128)} %param.23, s32[128,16]{0,1:T(8,128)} %param.20, s32[128,16]{0,1:T(8,128)} %param.19, s32[128,1]{0,1:T(1,128)} %bitcast.7), kind=kLoop, calls=%fused_computation | loop fusion | flops 15744 | bytes 41984 | tf_op jit(solution)/shard_map/concatenate | solution.py:714
  0.7 0.1 copy.18
  0.8 0.6 %pad.4.table_in = s32[136,41]{1,0:T(8,128)} pad(s32[128,41]{1,0:T(8,128)S(1)} %copy.18, s32[]{:T(128)} %constant.0.clone.1), padding=4_4x0_0 | pad | bytes 43300 | tf_op jit(solution)/shard_map/jit(_pad)/pad | solution.py:715
  1.5 48.3 %step.1 = f32[2,24,680]{2,1,0:T(8,128)} custom-call(f32[2,16,680]{2,1,0:T(8,128)} %coeffs.1, f32[3,16,768]{2,1,0:T(8,128)} %points_in.1, s32[6,16]{1,0:T(8,128)} %bitcast.6, f32[8,8]{1,0:T(8,128)} %reaction_in.1, f32[680,768]{1,0:T(8,128)} %bitcast.4, s32[136,41]{1,0:T(8,128)} %pad.4.table_in, bf16[2,680,680]{2,1,0:T(8,128)(2,1)} %near_in.1, ...), custom_call_target="tpu_custom_call" | custom-call | tf_op jit(solution)/shard_map/step/pallas_call | solution.py:664
  49.8 1.6 %copy.20 = f32[2,24,680]{2,1,0:T(8,128)} copy(f32[2,24,680]{2,1,0:T(8,128)} %step.1) | data formatting | bytes 261120

commit v4 on v3

--- a/solution.py
+++ b/solution.py
@@ -389,7 +389,6 @@
     lane = lax.broadcasted_iota(jnp.int32, (8, 128), 1)
     zero = jnp.zeros((8, 128), jnp.float32)
     full = width // 128
-    flat = dense.reshape(n * leaf_dev * species * ROWS, 128)
 
     def expand(slot):
         def chunk(c, carry):
@@ -407,11 +406,13 @@
                     )
                 x_high = x.astype(jnp.bfloat16).astype(jnp.float32)
                 tiles.append((x_high, x - x_high))
-            base = ((slot * leaf_dev + 8 * h) * species + s) * ROWS
             for g, (i, upper) in enumerate(GROUPS):
+                turned = []
                 for k in range(8):
                     j = 8 * upper + k
-                    if i + j <= ORDER:
+                    if i + j > ORDER:
+                        piece = zero
+                    else:
                         length = ORDER + 1 - i - j
                         t, shift = divmod(starts[i, j], 128)
                         parts = []
@@ -426,20 +427,13 @@
                             parts.append(part)
                         second = jnp.where((lane >= 16) & (lane < 16 + length), parts[1], zero)
                         piece = jnp.where(lane < length, parts[0], second)
-                        flat[pl.ds(base + 8 * g + k, 8, stride=species * ROWS), :] = piece
+                    turned.append(piece)
+                turned = pltpu.einshape("kln->lkn", jnp.stack(turned, axis=0))
+                dense[pl.ds(slot * leaf_dev + 8 * h, 8), pl.ds(pl.multiple_of(s * ROWS + 8 * g, 8), 8), :] = turned
             return carry
 
         lax.fori_loop(0, species * leaf_dev // 8, chunk, 0)
 
-    partial = [g for g, (i, upper) in enumerate(GROUPS) if i + 8 * upper + 7 > ORDER]
-
-    def clear(leaf, carry):
-        for s in range(species):
-            for g in partial:
-                dense[leaf, s * ROWS + 8 * g : s * ROWS + 8 * g + 8, :] = zero
-        return carry
-
-    lax.fori_loop(0, n * leaf_dev, clear, 0)
     loads[0].wait()
 
     def arrive(p, carry):

time: 51.6 us -> 50.2 us (0.973)
  Pallas kernels: 48.3 us -> 47 us
    pallas_call x1, Pallas kernels: 48.3 us -> 47 us  [whole_step(): pl.pallas_call(functools.partial(step_kernel, n, n_sp, pieces, near_count...]
where the time goes in v4:
time: 50.2 us; the launch traced here: 50 us
  Pallas kernels  47 us (94%)
  local copies, waits for them, and re-layouts  2.33 us (5%)
  other arithmetic  0.74 us (1%)
    pallas_call x1, Pallas kernels, whole_step(): pl.pallas_call(functools.partial(step_kernel, n, n_sp, pieces, near_count...  47 us
    unnamed x1, local copies, waits for them, and re-layouts  1.58 us

profile of v4, /device:TPU:0, one launch (start us, length us, event | category | flops | bytes accessed | tf_op | source)
XLA Modules:
  0.0 50.0 jit_solution(6995095787032929081)
XLA Ops:
  0.0 0.7 %pad_add_fusion = s32[128,41]{0,1:T(8,128)S(1)} fusion(s32[128,8]{0,1:T(8,128)} %param.23, s32[128,16]{0,1:T(8,128)} %param.20, s32[128,16]{0,1:T(8,128)} %param.19, s32[128,1]{0,1:T(1,128)} %bitcast.7), kind=kLoop, calls=%fused_computation | loop fusion | flops 15744 | bytes 41984 | tf_op jit(solution)/shard_map/concatenate | solution.py:708
  0.7 0.1 copy.18
  0.8 0.6 %pad.4.table_in = s32[136,41]{1,0:T(8,128)} pad(s32[128,41]{1,0:T(8,128)S(1)} %copy.18, s32[]{:T(128)} %constant.0.clone.1), padding=4_4x0_0 | pad | bytes 43300 | tf_op jit(solution)/shard_map/jit(_pad)/pad | solution.py:709
  1.5 47.0 %step.1 = f32[2,24,680]{2,1,0:T(8,128)} custom-call(f32[2,16,680]{2,1,0:T(8,128)} %coeffs.1, f32[3,16,768]{2,1,0:T(8,128)} %points_in.1, s32[6,16]{1,0:T(8,128)} %bitcast.6, f32[8,8]{1,0:T(8,128)} %reaction_in.1, f32[680,768]{1,0:T(8,128)} %bitcast.4, s32[136,41]{1,0:T(8,128)} %pad.4.table_in, bf16[2,680,680]{2,1,0:T(8,128)(2,1)} %near_in.1, ...), custom_call_target="tpu_custom_call" | custom-call | tf_op jit(solution)/shard_map/step/pallas_call | solution.py:658
  48.4 1.6 %copy.20 = f32[2,24,680]{2,1,0:T(8,128)} copy(f32[2,24,680]{2,1,0:T(8,128)} %step.1) | data formatting | bytes 261120

commit v5 on v4

--- a/solution.py
+++ b/solution.py
@@ -416,16 +416,17 @@
                         length = ORDER + 1 - i - j
                         t, shift = divmod(starts[i, j], 128)
                         parts = []
-                        for kind in range(2):
+                        for kind in range(3):
                             turn = (128 - shift + 16 * kind) % 128
-                            part = tiles[t][kind]
+                            part = tiles[t][kind % 2]
                             if turn:
                                 part = pltpu.roll(part, turn, 1)
                             if shift + length > 128:
-                                rest = pltpu.roll(tiles[t + 1][kind], turn, 1)
+                                rest = pltpu.roll(tiles[t + 1][kind % 2], turn, 1)
                                 part = jnp.where(lane < 128 - shift + 16 * kind, part, rest)
                             parts.append(part)
-                        second = jnp.where((lane >= 16) & (lane < 16 + length), parts[1], zero)
+                        third = jnp.where((lane >= 32) & (lane < 32 + length), parts[2], zero)
+                        second = jnp.where((lane >= 16) & (lane < 16 + length), parts[1], third)
                         piece = jnp.where(lane < length, parts[0], second)
                     turned.append(piece)
                 turned = pltpu.einshape("kln->lkn", jnp.stack(turned, axis=0))
@@ -497,19 +498,12 @@
 
     def block(b):
         leaf = owner[lax.div(b, leaf_dev), lax.rem(b, leaf_dev)]
-        lhs = dense[leaf][:, 0:32].astype(jnp.bfloat16)
+        lhs = dense[leaf][:, 0:48].astype(jnp.bfloat16)
         here = pl.ds(pl.multiple_of(b * 16, 16), 16)
         tx, ty, tz = cheb[0, here, :], cheb[1, here, :], cheb[2, here, :]
         tz_high = tz.astype(jnp.bfloat16).astype(jnp.float32)
-        rhs = jnp.concatenate(
-            [
-                jnp.concatenate([tz_high, tz - tz_high], axis=1),
-                jnp.concatenate([tz_high, jnp.zeros_like(tz)], axis=1),
-            ],
-            axis=0,
-        ).astype(jnp.bfloat16)
-        both = jnp.dot(lhs, rhs, preferred_element_type=jnp.float32)
-        inner = both[:, :PB] + both[:, PB:]
+        rhs = jnp.concatenate([tz_high, tz_high, tz - tz_high], axis=0).astype(jnp.bfloat16)
+        inner = jnp.dot(lhs, rhs, preferred_element_type=jnp.float32)
         for s in range(species):
             total = [None, None]
             for g, (i, upper) in enumerate(GROUPS):

time: 50.2 us -> 49.5 us (0.986)
  Pallas kernels: 47 us -> 46.3 us
    pallas_call x1, Pallas kernels: 47 us -> 46.3 us  [whole_step(): pl.pallas_call(functools.partial(step_kernel, n, n_sp, pieces, near_count...]
where the time goes in v5:
time: 49.5 us; the launch traced here: 49.3 us
  Pallas kernels  46.3 us (94%)
  local copies, waits for them, and re-layouts  2.33 us (5%)
  other arithmetic  0.74 us (1%)
    pallas_call x1, Pallas kernels, whole_step(): pl.pallas_call(functools.partial(step_kernel, n, n_sp, pieces, near_count...  46.3 us
    unnamed x1, local copies, waits for them, and re-layouts  1.58 us

profile of v5, /device:TPU:0, one launch (start us, length us, event | category | flops | bytes accessed | tf_op | source)
XLA Modules:
  0.0 49.3 jit_solution(14400847983603525224)
XLA Ops:
  0.0 0.7 %pad_add_fusion = s32[128,41]{0,1:T(8,128)S(1)} fusion(s32[128,8]{0,1:T(8,128)} %param.23, s32[128,16]{0,1:T(8,128)} %param.20, s32[128,16]{0,1:T(8,128)} %param.19, s32[128,1]{0,1:T(1,128)} %bitcast.7), kind=kLoop, calls=%fused_computation | loop fusion | flops 15744 | bytes 41984 | tf_op jit(solution)/shard_map/concatenate | solution.py:702
  0.7 0.1 copy.18
  0.8 0.6 %pad.4.table_in = s32[136,41]{1,0:T(8,128)} pad(s32[128,41]{1,0:T(8,128)S(1)} %copy.18, s32[]{:T(128)} %constant.0.clone.1), padding=4_4x0_0 | pad | bytes 43300 | tf_op jit(solution)/shard_map/jit(_pad)/pad | solution.py:703
  1.5 46.3 %step.1 = f32[2,24,680]{2,1,0:T(8,128)} custom-call(f32[2,16,680]{2,1,0:T(8,128)} %coeffs.1, f32[3,16,768]{2,1,0:T(8,128)} %points_in.1, s32[6,16]{1,0:T(8,128)} %bitcast.6, f32[8,8]{1,0:T(8,128)} %reaction_in.1, f32[680,768]{1,0:T(8,128)} %bitcast.4, s32[136,41]{1,0:T(8,128)} %pad.4.table_in, bf16[2,680,680]{2,1,0:T(8,128)(2,1)} %near_in.1, ...), custom_call_target="tpu_custom_call" | custom-call | tf_op jit(solution)/shard_map/step/pallas_call | solution.py:652
  47.7 1.6 %copy.20 = f32[2,24,680]{2,1,0:T(8,128)} copy(f32[2,24,680]{2,1,0:T(8,128)} %step.1) | data formatting | bytes 261120
